TPU v7x, 128 devices: a whole 4x4x4 slice. The times are simulated.
128 devices in a mesh: pos: 16 (over x, y), obj: 8 (over z, core).
Axes of the slice: x: 4, y: 4, z: 4, core: 2. Of those that a mesh axis runs over, the one named last changes fastest.
Arguments:
- object_field: float32 [2, 4096, 6144], P(None, 'obj', 'pos'), may hold values from -5 to 5
- probe: float32 [2, 256, 256], replicated, may hold values from -5 to 5
- amplitude: bfloat16 [2048, 256, 256], P(('pos', 'obj')), may hold values from 0.19921875 to 3
- row_offset: int32 [2048], P(('pos', 'obj')), may hold values from 0 to 256
- col_offset: int32 [2048], P(('pos', 'obj')), may hold values from 0 to 128
- owner: int32 [2048], P(('pos', 'obj')), may hold values from 0 to 15, as said below
Outputs:
- new_object: float32 [2, 4096, 6144], P(None, 'obj', 'pos')
- new_probe: float32 [2, 256, 256], replicated
Inputs may be any that keep to these rules, and one draw needn't show every extreme that they name: Among the 16 positions of one device no owner is named more than 2 times; in each row band one owner is named exactly 2 times by every device.
All inputs are finite; a program needn't handle non-finite values.
Results may differ from a plain program's by a relative error of at most 0.005.
The roundings to bfloat16 on the way count: a program that leaves them out, or rounds other values in their place, can miss the bound.
Values may be sent and summed in bfloat16 or wider, within the bound.
A program may use at most 128 MiB of HBM per device.

v0:
```python
import math

import jax
import jax.numpy as jnp
from jax import lax
from jax.sharding import PartitionSpec as P


def padded_2(block, sides, width):
    for axis, dim in sides:
        count = lax.axis_size(axis)
        forward = [(i, i + 1) for i in range(count - 1)]
        forward.append((count - 1, 0))
        backward = [(target, source) for source, target in forward]
        low = lax.ppermute(
            lax.slice_in_dim(block, block.shape[dim] - width, None, axis=dim), axis, forward
        )
        high = lax.ppermute(lax.slice_in_dim(block, 0, width, axis=dim), axis, backward)
        block = jnp.concatenate([low, block, high], axis=dim)
    return block


def dft_tables(size):
    index = jnp.arange(size, dtype=jnp.int32)
    product = index[:, None] * index[None, :] % size
    angle = product.astype(jnp.float32) * (2.0 * math.pi / size)
    scale = 1.0 / math.sqrt(size)
    real_part = (jnp.cos(angle) * scale).astype(jnp.bfloat16)
    imag_part = (-jnp.sin(angle) * scale).astype(jnp.bfloat16)
    return (real_part, imag_part)


def left_apply(mat_re, mat_im, val_re, val_im):

    def product(matrix, values):
        return jnp.einsum("jk,bkl->bjl", matrix, values, preferred_element_type=jnp.float32)

    return (
        product(mat_re, val_re) - product(mat_im, val_im),
        product(mat_re, val_im) + product(mat_im, val_re),
    )


def right_apply(val_re, val_im, mat_re, mat_im):

    def product(values, matrix):
        return jnp.einsum("bjk,kl->bjl", values, matrix, preferred_element_type=jnp.float32)

    return (
        product(val_re, mat_re) - product(val_im, mat_im),
        product(val_re, mat_im) + product(val_im, mat_re),
    )


def position_terms(patches, amps, validity, probe, tables):
    four_re, four_im, conj_im = tables
    patch_re = patches[:, 0].astype(jnp.float32)
    patch_im = patches[:, 1].astype(jnp.float32)
    probe_re = probe[0]
    probe_im = probe[1]
    psi_re = (probe_re * patch_re - probe_im * patch_im).astype(jnp.bfloat16)
    psi_im = (probe_re * patch_im + probe_im * patch_re).astype(jnp.bfloat16)
    left_re, left_im = left_apply(four_re, four_im, psi_re, psi_im)
    wave_re, wave_im = right_apply(
        left_re.astype(jnp.bfloat16), left_im.astype(jnp.bfloat16), four_re, four_im
    )
    magnitude = jnp.sqrt(wave_re * wave_re + wave_im * wave_im)
    factor = 1.0 - amps.astype(jnp.float32) / jnp.maximum(magnitude, 0.5)
    diff_re = (wave_re * factor).astype(jnp.bfloat16)
    diff_im = (wave_im * factor).astype(jnp.bfloat16)
    back_re, back_im = left_apply(four_re, conj_im, diff_re, diff_im)
    chi_re, chi_im = right_apply(
        back_re.astype(jnp.bfloat16), back_im.astype(jnp.bfloat16), four_re, conj_im
    )
    chi_re = chi_re * validity[:, None, None]
    chi_im = chi_im * validity[:, None, None]
    grad_re = (probe_re * chi_re + probe_im * chi_im).astype(jnp.bfloat16)
    grad_im = (probe_re * chi_im - probe_im * chi_re).astype(jnp.bfloat16)
    term_re = jnp.sum(patch_re * chi_re + patch_im * chi_im, axis=0)
    term_im = jnp.sum(patch_re * chi_im - patch_im * chi_re, axis=0)
    return (jnp.stack([grad_re, grad_im], axis=1), jnp.stack([term_re, term_im]))


def run_terms(patches, amps, validity, probe, tables):
    count = patches.shape[0]
    size = patches.shape[2]
    batch_size = math.gcd(count, 8)
    groups = count // batch_size
    grouped = (
        patches.reshape(groups, batch_size, 2, size, size),
        amps.reshape(groups, batch_size, size, size),
        validity.reshape(groups, batch_size),
    )
    grads, terms = lax.map(
        lambda items: position_terms(items[0], items[1], items[2], probe, tables), grouped
    )
    return (grads.reshape(count, 2, size, size), jnp.sum(terms, axis=0))


def extract(tile, corners, size):
    zero = jnp.zeros((), jnp.int32)
    windows = jax.vmap(lambda row, col: lax.dynamic_slice(tile, (zero, row, col), (2, size, size)))(
        corners[:, 0], corners[:, 1]
    )
    return windows.astype(jnp.bfloat16)


def add_scaled(start_value, grads, corners, size):
    zero = jnp.zeros((), jnp.int32)

    def add_one(item, acc):
        corner = (zero, corners[item, 0], corners[item, 1])
        window = lax.dynamic_slice(acc, corner, (2, size, size))
        return lax.dynamic_update_slice(
            acc, window - 0.25 * grads[item].astype(jnp.float32), corner
        )

    return lax.fori_loop(0, grads.shape[0], add_one, start_value)


def shards(object_field, probe, amplitude, row_offset, col_offset, owner):
    n_pos = lax.axis_size("pos")
    n_obj = lax.axis_size("obj")
    pos_dev = amplitude.shape[0]
    size = amplitude.shape[1]
    capacity = max(2, pos_dev // n_pos + 1)
    slots = n_pos * capacity
    padded = padded_2(object_field.astype(jnp.bfloat16), (("pos", 2), ("obj", 1)), 1).astype(
        object_field.dtype
    )
    smooth = 4.0 * object_field - padded[:, :-2, 1:-1] - padded[:, 2:, 1:-1]
    smooth = smooth - padded[:, 1:-1, :-2] - padded[:, 1:-1, 2:]
    four_re, four_im = dft_tables(size)
    tables = (four_re, four_im, -four_im)
    onehot = (owner[:, None] == jnp.arange(n_pos, dtype=jnp.int32)[None, :]).astype(jnp.int32)
    earlier = jnp.cumsum(onehot, axis=0) - onehot
    ranking = jnp.sum(earlier * onehot, axis=1)
    target = owner * capacity + ranking
    matching = (target[:, None] == jnp.arange(slots, dtype=jnp.int32)[None, :]).astype(jnp.int32)
    source = jnp.sum(matching * jnp.arange(pos_dev, dtype=jnp.int32)[:, None], axis=0)
    filled = jnp.sum(matching, axis=0) > 0
    listing = jnp.stack([row_offset, col_offset, jnp.ones_like(row_offset)], axis=1)
    slot_info = jnp.where(filled[:, None], listing[source], 0).reshape(n_pos, capacity, 3)
    received = lax.all_to_all(slot_info, "pos", split_axis=0, concat_axis=0, tiled=True)
    items = received.shape[1]
    windows = extract(object_field, received.reshape(-1, 3), size)
    windows = windows.reshape(n_pos, items, 2, size, size)
    fetched = lax.all_to_all(windows, "pos", split_axis=0, concat_axis=0, tiled=True)
    mine = fetched.reshape(slots, 2, size, size)[target]
    grads, probe_part = run_terms(mine, amplitude, jnp.ones((pos_dev,), jnp.float32), probe, tables)
    grad_slots = jnp.where(filled[:, None, None, None], grads[source], jnp.zeros((), jnp.bfloat16))
    incoming = lax.all_to_all(
        grad_slots.reshape(n_pos, capacity, 2, size, size),
        "pos",
        split_axis=0,
        concat_axis=0,
        tiled=True,
    )
    incoming = incoming.reshape(slots, 2, size, size)
    corners = received.reshape(slots, 3)
    base = object_field - 0.125 * smooth
    new_object = add_scaled(base, incoming, corners, size)
    probe_grad = lax.psum(probe_part, ("pos", "obj"))
    n_total = pos_dev * n_pos * n_obj
    new_probe = probe - probe_grad * (1.0 / math.sqrt(n_total))
    return (new_object, new_probe)


def solution(mesh):
    placed = (
        P(None, "obj", "pos"),
        P(),
        P(("pos", "obj"), None, None),
        P(("pos", "obj")),
        P(("pos", "obj")),
        P(("pos", "obj")),
    )
    return jax.shard_map(
        shards, mesh=mesh, in_specs=placed, out_specs=(P(None, "obj", "pos"), P()), check_vma=False
    )
```

profile of v0, /device:TPU:1, one launch (start us, length us, event | category | flops | bytes accessed | tf_op | source)
XLA Modules:
  0.0 1000.2 jit_solution(17226852778361089383)
XLA Ops:
  12.1 7.6 all-to-all-start
  21.2 4.9 all-to-all-done
  26.3 89.1 %while.29 = (s32[]{:T(128)}, bf16[2,512,384]{2,1,0:T(8,128)(2,1)S(1)}, s32[32,3]{0,1:T(4,128)S(1)}, bf16[32,2,256,256]{3,2,1,0:T(8,128)(2,1)}, s32[]{:T(128)}) while((s32[]{:T(128)}, bf16[2,512,384]{2,1,0:T(8,128)(2,1)S(1)}, s32[32,3]{0,1:T(4,128)S(1)}, bf16[32,2,256,256]{3,2,1,0:T(8,128)(2,1)}, s32[]{:T(128)}) %tuple.89), condition=%wide.while_cond, body=%wide.while_body.sunk | while | flops 2 | bytes 525929 | solution.py:102
  26.9 2.2 bitcast_dynamic-update-slice_fusion.2
  29.7 2.2 bitcast_dynamic-update-slice_fusion.2
  32.5 2.2 bitcast_dynamic-update-slice_fusion.2
  49.2 2.2 bitcast_dynamic-update-slice_fusion.2
  52.0 2.2 bitcast_dynamic-update-slice_fusion.2
  74.3 2.2 bitcast_dynamic-update-slice_fusion.2
  85.4 2.2 bitcast_dynamic-update-slice_fusion.2
  93.8 2.2 bitcast_dynamic-update-slice_fusion.2
  104.9 2.2 bitcast_dynamic-update-slice_fusion.2
  107.7 2.2 bitcast_dynamic-update-slice_fusion.2
  116.3 4.7 all-to-all-start.1
  121.1 131.1 %all-to-all-done.1 = bf16[16,2,2,256,256]{4,3,2,1,0:T(8,128)(2,1)} async-done(((bf16[16,2,2,256,256]{4,3,2,1,0:T(8,128)(2,1)}), bf16[16,2,2,256,256]{4,3,2,1,0:T(8,128)(2,1)}, u32[]{:S(2)}, u32[]{:S(2)}) %all-to-all-start.1) | async-done | bytes 8388640 | tf_op jit(solution)/shard_map/all_to_all | solution.py:148
  252.2 6.2 gather_fusion.1
  258.4 60.2 %while.30 = (s32[]{:T(128)}, bf16[2,8,2,256,256]{4,3,2,1,0:T(8,128)(2,1)}, f32[2,2,256,256]{3,2,1,0:T(8,128)S(1)}, f32[2,256,256]{2,1,0:T(8,128)S(1)}, bf16[2,8,...) while((s32[]{:T(128)}, ...), condition=%wide.region_7.8_spmd.clone.clone, body=%wide.region_4.7_spmd.clone.clone.sunk | while | flops 4348182528 | bytes 96470128 | solution.py:94
  271.3 2.8 multiply_convert_fusion.9
  283.9 3.0 fusion.253
  301.3 2.8 multiply_convert_fusion.9
  314.0 3.0 fusion.253
  318.6 7.5 gather_fusion.2
  326.1 7.2 broadcast_select_fusion
  333.3 8.7 all-to-all-start.2
  343.6 3.5 collective-permute-start.1
  347.1 96.5 %collective-permute-done = bf16[2,512,1]{2,1,0:T(8,128)(2,1)S(1)} collective-permute-done((bf16[2,512,1]{2,1,0:T(8,128)(2,1)S(1)}, bf16[2,512,1]{2,1,0:T(8,128)(2,1)S(1)}, u32[]{:S(2)}, u32[]{:S(2)}) %collective-permute-start) | collective-permute-done | bytes 2080 | tf_op jit(solution)/shard_map/ppermute | solution.py:15
  443.6 3.9 collective-permute-done.1
  448.2 5.8 collective-permute-start.2
  454.8 2.3 collective-permute-done.3
  461.1 3.9 fusion.143
  465.0 146.4 %all-reduce.2.cloned.1.call-done = f32[2,256,256]{2,1,0:T(8,128)} async-done(((f32[2,256,256]{2,1,0:T(8,128)}), f32[2,256,256]{2,1,0:T(8,128)}) %all-reduce.2.cloned.1.call-update) | async-done | bytes 524304 | tf_op jit(solution)/shard_map/psum | solution.py:163
  613.3 380.1 %while.28 = (s32[]{:T(128)}, f32[2,512,384]{2,1,0:T(8,128)}, s32[32,3]{0,1:T(4,128)S(1)}, bf16[32,2,256,256]{3,2,1,0:T(8,128)(2,1)}, s32[]{:T(128)}, /*index=5*/s32[]{:T(128)}, s32[]{:T(128)}, s32[]{:T(128)}) while((s32[]{:T(128)}, f32[2,512,384]{2,1,0:T(8,128)}, s32[32,3]{0,1:T(4,128)S(1)}, bf16[32,2,256,256]{3,2,1,0:T(8,128)(2,1)}, ...), condition=%wide.region_9.10_spmd, body=%wide.region_8.9_spmd.sunk | while | flops 393224 | bytes 2359485 | solution.py:118
  619.1 6.2 dynamic_update_slice.24
  631.2 5.7 dynamic_update_slice.24
  642.8 5.7 dynamic_update_slice.24
  654.4 5.7 dynamic_update_slice.24
  666.0 6.0 dynamic_update_slice.24
  677.9 5.7 dynamic_update_slice.24
  689.5 6.4 dynamic_update_slice.24
  701.7 5.7 dynamic_update_slice.24
  713.3 6.4 dynamic_update_slice.24
  725.6 5.7 dynamic_update_slice.24
  737.2 6.1 dynamic_update_slice.24
  749.2 6.0 dynamic_update_slice.24
  761.1 6.5 dynamic_update_slice.24
  773.5 5.7 dynamic_update_slice.24
  785.0 6.1 dynamic_update_slice.24
  797.0 5.7 dynamic_update_slice.24
  808.6 6.4 dynamic_update_slice.24
  820.8 5.7 dynamic_update_slice.24
  832.4 6.3 dynamic_update_slice.24
  844.6 6.5 dynamic_update_slice.24
  856.9 6.2 dynamic_update_slice.24
  869.0 5.7 dynamic_update_slice.24
  880.6 6.2 dynamic_update_slice.24
  892.6 5.7 dynamic_update_slice.24
  904.2 6.4 dynamic_update_slice.24
  916.5 5.7 dynamic_update_slice.24
  928.1 6.3 dynamic_update_slice.24
  940.3 5.7 dynamic_update_slice.24
  951.9 6.2 dynamic_update_slice.24
  964.0 5.7 dynamic_update_slice.24
  975.5 6.2 dynamic_update_slice.24
  987.6 5.7 dynamic_update_slice.24
  (242 shorter events, 198.4 us)
Async XLA Ops:
  12.1 14.0 %all-to-all-start = ((s32[16,2,3]{2,1,0:T(2,128)}), s32[16,2,3]{2,1,0:T(2,128)S(1)}, u32[]{:S(2)}, u32[]{:S(2)}) async-start(s32[16,2,3]{2,1,0:T(2,128)} %copy.88), calls=%async_computation | async-start | bytes 32768 | tf_op jit(solution)/shard_map/all_to_all | solution.py:144
  26.3 89.2 %copy-start.6 = (s32[32,3]{0,1:T(4,128)}, s32[32,3]{0,1:T(4,128)S(1)}, u32[]{:S(2)}) copy-start(s32[32,3]{0,1:T(4,128)S(1)} %copy.109) | copy-start | bytes 1156
  115.4 0.9 copy-start
  116.3 135.9 %all-to-all-start.1 = ((bf16[16,2,2,256,256]{4,3,2,1,0:T(8,128)(2,1)}), bf16[16,2,2,256,256]{4,3,2,1,0:T(8,128)(2,1)}, u32[]{:S(2)}, u32[]{:S(2)}) async-start(bf16[16,2,2,256,256]{4,3,2,1,0:T(8,128)(2,1)} %bitcast.241), calls=%async_computation.1 | async-start | bytes 16777216 | tf_op jit(solution)/shard_map/all_to_all | solution.py:148
  252.2 6.2 copy-start.2
  269.7 1.6 copy-start.8
  299.7 1.6 copy-start.8
  318.6 7.5 copy-start.3
  333.3 8.8 copy-start.1
  333.3 279.9 %all-to-all-start.2 = ((bf16[16,2,2,256,256]{4,3,2,1,0:T(8,128)(2,1)}), bf16[16,2,2,256,256]{4,3,2,1,0:T(8,128)(2,1)}, u32[]{:S(2)}, u32[]{:S(2)}) async-start(bf16[16,2,2,256,256]{4,3,2,1,0:T(8,128)(2,1)} %broadcast_select_fusion), calls=%async_computation.2 | async-start | bytes 16777216 | tf_op jit(solution)/shard_map/all_to_all | solution.py:152
  342.1 269.3 %all-reduce.2.cloned.1.call-start = ((), (), s32[]{:S(2)}) async-start(), calls=%async_computation.3 | async-start | bytes 1048576 | tf_op jit(solution)/shard_map/psum | solution.py:163
  342.3 101.3 %collective-permute-start = (bf16[2,512,1]{2,1,0:T(8,128)(2,1)S(1)}, bf16[2,512,1]{2,1,0:T(8,128)(2,1)S(1)}, u32[]{:S(2)}, u32[]{:S(2)}) collective-permute-start(bf16[2,512,1]{2,1,0:T(8,128)(2,1)S(1)} %get-tuple-element.301), channel_id=1, source_target_pairs={{0,8},{8,16},{16,24},{24,32},{32,40},{40,48},{48,56},{56,64},{64,7... | collective-permute-start | bytes 6152 | tf_op jit(solution)/shard_map/ppermute | solution.py:15
  343.6 103.9 %collective-permute-start.1 = (bf16[2,512,1]{2,1,0:T(8,128)(2,1)S(1)}, bf16[2,512,1]{2,1,0:T(8,128)(2,1)S(1)}, u32[]{:S(2)}, u32[]{:S(2)}) collective-permute-start(bf16[2,512,1]{2,1,0:T(8,128)(2,1)S(1)} %get-tuple-element.302), channel_id=1, source_target_pairs={{8,0},{16,8},{24,16},{32,24},{40,32},{48,40},{56,48},{64,56},{72,6... | collective-permute-start | bytes 6152 | tf_op jit(solution)/shard_map/ppermute | solution.py:18
  443.6 3.9 copy-start.4
  447.5 0.7 copy-start.5
  448.2 6.6 collective-permute-start.2
  454.0 3.0 collective-permute-start.3
  461.0 152.2 %copy-start.7 = (s32[32,3]{0,1:T(4,128)S(1)}, s32[32,3]{0,1:T(4,128)}, u32[]{:S(2)}) copy-start(s32[32,3]{0,1:T(4,128)} %copy-done.6) | copy-start | bytes 1156
Sparse Core Ops, SparseCore 0:
  461.2 150.1 all-reduce.1
where the time goes:
time: 1020 us; the launch traced here: 1000 us
  waiting for transfers between devices  386 us (38%)
  local copies, waits for them, and re-layouts  324 us (32%)
  loops' own time  122 us (12%)
  other arithmetic  70.1 us (7%)
  matrix products  53 us (5%)
  starting transfers between devices  31.8 us (3%)
  between operations  14.2 us (1%)
    dynamic_update_slice x32, local copies, waits for them, and re-layouts, add_one(): lax.dynamic_update_slice(acc, window - 0.25 * grads[item].astype(jnp.floa...  192 us
    psum x1, waiting for transfers between devices, shards(): probe_grad = lax.psum(probe_part, ('pos', 'obj'))  146 us
    all_to_all x1, waiting for transfers between devices, shards(): lax.all_to_all(windows, 'pos', split_axis=0, concat_axis=0, tiled=True)  131 us
    another operation x1, loops' own time, add_scaled(): return lax.fori_loop(0, grads.shape[0], add_one, start_value)  121 us
    ppermute x2, waiting for transfers between devices, padded_2(): lax.ppermute(lax.slice_in_dim(block, block.shape[dim] - width, None, axis...  97.2 us
    gather x96, local copies, waits for them, and re-layouts  89.1 us
    sub x32, other arithmetic, add_one(): window - 0.25 * grads[item].astype(jnp.float32)  45.3 us
    dot_general x16, matrix products, product(): jnp.einsum('bjk,kl->bjl', values, matrix, preferred_element_type=jnp.floa...  28.6 us
  transfers between devices with their start and end apart: 8, of which 7 were waited for; matrix products, arithmetic and copies ran while one was open for 1% of the time, Pallas kernels for 0%

commit v1 on v0

v1 whole, which is shorter than its diff:
```python
import functools
import math

import jax
import jax.numpy as jnp
import numpy as np
from jax import lax
from jax.experimental import pallas as pl
from jax.experimental.pallas import tpu as pltpu
from jax.sharding import PartitionSpec as P

SIZE = 256
CAPACITY = 2
LANES = 128
F32 = jnp.float32
BF16 = jnp.bfloat16


def dft_blocks():
    index = np.arange(SIZE, dtype=np.int64)
    product = (index[:, None] * index[None, :]) % SIZE
    angle = product.astype(np.float32) * np.float32(2.0 * math.pi / SIZE)
    scale = 1.0 / math.sqrt(SIZE)
    real = (np.cos(angle.astype(np.float64)) * scale).astype(np.float32)
    imag = (-np.sin(angle.astype(np.float64)) * scale).astype(np.float32)
    real = jnp.asarray(real).astype(BF16)
    imag = jnp.asarray(imag).astype(BF16)
    top = jnp.concatenate([real, -imag], axis=1)
    bottom = jnp.concatenate([imag, real], axis=1)
    left = jnp.concatenate([top, bottom], axis=0)
    top = jnp.concatenate([real, imag], axis=1)
    bottom = jnp.concatenate([-imag, real], axis=1)
    return left, jnp.concatenate([top, bottom], axis=0)


def pack_kernel(n_pos, owner, rows, cols, amps, slots, meta, source, count, sems):
    total = n_pos * CAPACITY
    n_dev = owner.shape[0]

    @pl.loop(0, n_pos)
    def _(i):
        count[i] = 0

    @pl.loop(0, total)
    def _(i):
        source[i] = 0
        meta[i, 0] = 2 * SIZE
        meta[i, 1] = 0

    @pl.loop(0, n_dev)
    def _(i):
        o = owner[i]
        k = count[o]
        count[o] = k + 1
        slot = k * n_pos + o
        source[slot] = i
        meta[slot, 0] = rows[i]
        meta[slot, 1] = cols[i]

    @pl.loop(0, total)
    def _(i):
        pltpu.make_async_copy(amps.at[source[i]], slots.at[i], sems.at[i]).start()

    @pl.loop(0, total)
    def _(i):
        pltpu.make_async_copy(amps.at[source[i]], slots.at[i], sems.at[i]).wait()


def pack(owner, rows, cols, amps, n_pos):
    total = n_pos * CAPACITY
    smem = pl.BlockSpec(memory_space=pltpu.SMEM)
    hbm = pl.BlockSpec(memory_space=pl.ANY)
    return pl.pallas_call(
        functools.partial(pack_kernel, n_pos),
        out_shape=(
            jax.ShapeDtypeStruct((total, SIZE, SIZE), BF16),
            jax.ShapeDtypeStruct((total, 2), jnp.int32),
        ),
        in_specs=[smem, smem, smem, hbm],
        out_specs=(hbm, smem),
        scratch_shapes=[
            pltpu.SMEM((total,), jnp.int32),
            pltpu.SMEM((n_pos,), jnp.int32),
            pltpu.SemaphoreType.DMA((total,)),
        ],
        name="pack",
    )(owner, rows, cols, amps)


STRIP = 32


def extract(meta_row, meta_col, tile, probe, window, psi, j):
    lane = lax.broadcasted_iota(jnp.int32, (STRIP, LANES), 1)
    first = lane < LANES - meta_col
    shift = lax.rem(LANES - meta_col, LANES)
    for s in range(0, SIZE, STRIP):
        parts = []
        for p in range(2):
            t = [
                pltpu.roll(tile[p, k, pl.ds(meta_row + s, STRIP), :], shift, 1)
                for k in range(3)
            ]
            parts.append([jnp.where(first, t[k], t[k + 1]) for k in range(2)])
        for k in range(2):
            cols = slice(k * LANES, (k + 1) * LANES)
            x_re, x_im = parts[0][k], parts[1][k]
            window[j, 0, s : s + STRIP, cols] = x_re
            window[j, 1, s : s + STRIP, cols] = x_im
            p_re = probe[0, s : s + STRIP, cols]
            p_im = probe[1, s : s + STRIP, cols]
            out = slice(j * SIZE + k * LANES, j * SIZE + (k + 1) * LANES)
            psi[s : s + STRIP, out] = (p_re * x_re - p_im * x_im).astype(BF16)
            psi[SIZE + s : SIZE + s + STRIP, out] = (p_re * x_im + p_im * x_re).astype(BF16)


def turn(value, out):
    for j in range(2):
        for part in range(2):
            out[j * SIZE : (j + 1) * SIZE, part * SIZE : (part + 1) * SIZE] = value[
                part * SIZE : (part + 1) * SIZE, j * SIZE : (j + 1) * SIZE
            ].astype(BF16)


def modulus(wave, amp, diff, j):
    for s in range(0, SIZE, STRIP):
        rows = slice(j * SIZE + s, j * SIZE + s + STRIP)
        w_re = wave[rows, 0:SIZE]
        w_im = wave[rows, SIZE : 2 * SIZE]
        a = amp[j, s : s + STRIP, :].astype(F32)
        power = w_re * w_re + w_im * w_im
        factor = 1.0 - a * lax.rsqrt(jnp.maximum(power, 0.25))
        cols = slice(j * SIZE, (j + 1) * SIZE)
        diff[s : s + STRIP, cols] = (w_re * factor).astype(BF16)
        diff[SIZE + s : SIZE + s + STRIP, cols] = (w_im * factor).astype(BF16)


def gather_back(meta_row, meta_col, chi, probe, window, acc, term, j):
    lane = lax.broadcasted_iota(jnp.int32, (STRIP, LANES), 1)
    later = lane >= meta_col
    shift = lax.rem(meta_col, LANES)
    row = jnp.bitwise_and(meta_row, 2 * SIZE - 1)
    zero = jnp.zeros((STRIP, LANES), F32)
    for s in range(0, SIZE, STRIP):
        rows = slice(j * SIZE + s, j * SIZE + s + STRIP)
        turned = [[], []]
        for k in range(2):
            cols = slice(k * LANES, (k + 1) * LANES)
            c_re = chi[rows, k * LANES : (k + 1) * LANES]
            c_im = chi[rows, SIZE + k * LANES : SIZE + (k + 1) * LANES]
            x_re = window[j, 0, s : s + STRIP, cols]
            x_im = window[j, 1, s : s + STRIP, cols]
            term[0, s : s + STRIP, cols] += x_re * c_re + x_im * c_im
            term[1, s : s + STRIP, cols] += x_re * c_im - x_im * c_re
            p_re = probe[0, s : s + STRIP, cols]
            p_im = probe[1, s : s + STRIP, cols]
            g_re = (p_re * c_re + p_im * c_im).astype(BF16).astype(F32)
            g_im = (p_re * c_im - p_im * c_re).astype(BF16).astype(F32)
            turned[0].append(pltpu.roll(g_re, shift, 1))
            turned[1].append(pltpu.roll(g_im, shift, 1))
        for p in range(2):
            low, high = turned[p]
            here = pl.ds(row + s, STRIP)
            acc[p, 0, here, :] += jnp.where(later, low, zero)
            acc[p, 1, here, :] += jnp.where(later, high, low)
            acc[p, 2, here, :] += jnp.where(later, zero, high)


def compute_kernel(
    first_call, last_call, n_steps,
    meta, obj, probe, left, right, amp, acc_in, term_in, base,
    out, term, tile, window, psi, half, wave, diff, chi, acc,
):
    step = pl.program_id(0)

    @pl.when(step == 0)
    def _():
        for p in range(2):
            for k in range(3):
                cols = slice(k * LANES, (k + 1) * LANES)
                tile[p, k, 0 : 2 * SIZE, :] = obj[p, :, cols].astype(BF16).astype(F32)
                tile[p, k, 2 * SIZE : 3 * SIZE, :] = jnp.zeros((SIZE, LANES), F32)
        if first_call:
            acc[...] = jnp.zeros_like(acc)
            term[...] = jnp.zeros_like(term)
        else:
            acc[...] = acc_in[...]
            term[...] = term_in[...]

    row = [meta[2 * step + j, 0] for j in range(2)]
    col = [meta[2 * step + j, 1] for j in range(2)]

    @pl.when(jnp.minimum(row[0], row[1]) < 2 * SIZE)
    def _():
        for j in range(2):
            extract(row[j], col[j], tile, probe, window, psi, j)
        turn(jnp.dot(left[...], psi[...], preferred_element_type=F32), half)
        wave[...] = jnp.dot(half[...], right[...], preferred_element_type=F32)
        for j in range(2):
            modulus(wave, amp, diff, j)
        turn(jnp.dot(right[...], diff[...], preferred_element_type=F32), half)
        chi[...] = jnp.dot(half[...], left[...], preferred_element_type=F32)
        for j in range(2):
            gather_back(row[j], col[j], chi, probe, window, acc, term, j)

    @pl.when(step == n_steps - 1)
    def _():
        if last_call:
            for p in range(2):
                for k in range(3):
                    cols = slice(k * LANES, (k + 1) * LANES)
                    out[p, :, cols] = base[p, :, cols] - 0.25 * acc[p, k]
        else:
            out[...] = acc[...]


def compute(first_call, last_call, meta, obj, probe, left, right, amp, acc_in, term_in, base):
    count = amp.shape[0]
    n_steps = count // 2
    whole = lambda *shape: pl.BlockSpec(shape, lambda i: (0,) * len(shape))
    dummy = pl.BlockSpec(memory_space=pl.ANY)
    panels = (2, 3, 2 * SIZE, LANES)
    acc_spec = dummy if first_call else whole(*panels)
    term_spec = dummy if first_call else whole(2, SIZE, SIZE)
    base_spec = whole(*obj.shape) if last_call else dummy
    out_shape = obj.shape if last_call else panels
    flops = count * 16 * 2 * SIZE**3
    return pl.pallas_call(
        functools.partial(compute_kernel, first_call, last_call, n_steps),
        grid=(n_steps,),
        out_shape=(
            jax.ShapeDtypeStruct(out_shape, F32),
            jax.ShapeDtypeStruct((2, SIZE, SIZE), F32),
        ),
        in_specs=[
            pl.BlockSpec(memory_space=pltpu.SMEM),
            whole(*obj.shape),
            whole(2, SIZE, SIZE),
            whole(2 * SIZE, 2 * SIZE),
            whole(2 * SIZE, 2 * SIZE),
            pl.BlockSpec((2, SIZE, SIZE), lambda i: (i, 0, 0)),
            acc_spec,
            term_spec,
            base_spec,
        ],
        out_specs=(whole(*out_shape), whole(2, SIZE, SIZE)),
        scratch_shapes=[
            pltpu.VMEM((2, 3, 3 * SIZE, LANES), F32),
            pltpu.VMEM((2, 2, SIZE, SIZE), F32),
            pltpu.VMEM((2 * SIZE, 2 * SIZE), BF16),
            pltpu.VMEM((2 * SIZE, 2 * SIZE), BF16),
            pltpu.VMEM((2 * SIZE, 2 * SIZE), F32),
            pltpu.VMEM((2 * SIZE, 2 * SIZE), BF16),
            pltpu.VMEM((2 * SIZE, 2 * SIZE), F32),
            pltpu.VMEM(panels, F32),
        ],
        compiler_params=pltpu.CompilerParams(
            dimension_semantics=("arbitrary",), vmem_limit_bytes=56 << 20
        ),
        cost_estimate=pl.CostEstimate(flops=flops, bytes_accessed=16 << 20, transcendentals=0),
        name="positions",
    )(meta, obj, probe, left, right, amp, acc_in, term_in, base)


def exchanged(block, axis, dim):
    count = lax.axis_size(axis)
    forward = [(i, (i + 1) % count) for i in range(count)]
    backward = [(target, source) for source, target in forward]
    size = block.shape[dim]
    low = lax.ppermute(lax.slice_in_dim(block, size - 1, size, axis=dim), axis, forward)
    high = lax.ppermute(lax.slice_in_dim(block, 0, 1, axis=dim), axis, backward)
    return jnp.concatenate([low, block, high], axis=dim)


def shards(object_field, probe, amplitude, row_offset, col_offset, owner):
    n_pos = lax.axis_size("pos")
    n_obj = lax.axis_size("obj")
    pos_dev = amplitude.shape[0]
    left, right = dft_blocks()
    slots, meta = pack(owner, row_offset, col_offset, amplitude, n_pos)
    arrived = [
        lax.all_to_all(slots[k * n_pos : (k + 1) * n_pos], "pos", 0, 0, tiled=True)
        for k in range(CAPACITY)
    ]
    corners = lax.all_to_all(meta.reshape(CAPACITY, n_pos, 2), "pos", 1, 1, tiled=True)
    tall = exchanged(object_field, "obj", 1)
    wide = exchanged(object_field, "pos", 2)
    smooth = 4.0 * object_field - tall[:, :-2] - tall[:, 2:] - wide[:, :, :-2] - wide[:, :, 2:]
    base = object_field - 0.125 * smooth
    none = jnp.zeros((8, 128), F32)
    acc, term = compute(
        True, False, corners[0], object_field, probe, left, right, arrived[0], none, none, none
    )
    new_object, term = compute(
        False, True, corners[1], object_field, probe, left, right, arrived[1], acc, term, base
    )
    probe_grad = lax.psum(term, ("pos", "obj"))
    n_total = pos_dev * n_pos * n_obj
    return new_object, probe - probe_grad * (1.0 / math.sqrt(n_total))


def solution(mesh):
    placed = (
        P(None, "obj", "pos"),
        P(),
        P(("pos", "obj"), None, None),
        P(("pos", "obj")),
        P(("pos", "obj")),
        P(("pos", "obj")),
    )
    return jax.shard_map(
        shards, mesh=mesh, in_specs=placed, out_specs=(P(None, "obj", "pos"), P()), check_vma=False
    )
```

time: 1020 us -> 432 us (0.42); the launches traced: 1000 us -> 431 us
  local copies, waits for them, and re-layouts: 324 us -> 8.69 us
  waiting for transfers between devices: 386 us -> 185 us
  Pallas kernels: 0 us -> 167 us
  loops' own time: 122 us -> 0 us
  other arithmetic: 70.1 us -> 4.06 us
  matrix products: 53 us -> 0 us
  blocking collectives: 0 us -> 29.8 us
    dynamic_update_slice x32 -> x0, local copies, waits for them, and re-layouts: 192 us -> none  [add_one(): lax.dynamic_update_slice(acc, window - 0.25 * grads[item].astype(jnp.floa...]
    pallas_call x0 -> x3, Pallas kernels: none -> 167 us  [the longest x1 130 us: pack(): pl.pallas_call(functools.partial(pack_kernel, n_pos), out_shape=(jax.Shap...]
    all_to_all x3 -> x2, waiting for transfers between devices: 136 us -> 2.51 us  [the longest x1 2.51 us: shards(): lax.all_to_all(meta.reshape(CAPACITY, n_pos, 2), 'pos', 1, 1, tiled=True)]
    another operation x3 -> x0, loops' own time: 122 us -> none  [the longest x1 121 us: add_scaled(): return lax.fori_loop(0, grads.shape[0], add_one, start_value)]
    gather x100 -> x0, local copies, waits for them, and re-layouts: 104 us -> none
    ppermute x4, waiting for transfers between devices: 103 us -> 25.5 us  [the longest x2 23.8 us: exchanged(): lax.ppermute(lax.slice_in_dim(block, size - 1, size, axis=dim), axis, for...]
    dot_general x32 -> x0, matrix products: 53 us -> none  [the longest x16 28.6 us: product(): jnp.einsum('bjk,kl->bjl', values, matrix, preferred_element_type=jnp.floa...]
    sub x33 -> x1, other arithmetic: 47.2 us -> 1.9 us  [shards(): return (new_object, probe - probe_grad * (1.0 / math.sqrt(n_total)))]
  transfers between devices with their start and end apart: 8 -> 7, of which waited for: 7 -> 4; matrix products, arithmetic and copies ran while one was open for 1% -> 2% of each run, Pallas kernels for 0% -> 5%
where the time goes in v1:
time: 432 us; the launch traced here: 431 us
  waiting for transfers between devices  185 us (43%)
  Pallas kernels  167 us (39%)
  blocking collectives  29.8 us (7%)
  starting transfers between devices  22.6 us (5%)
  between operations  14.1 us (3%)
  local copies, waits for them, and re-layouts  8.69 us (2%)
    psum x1, waiting for transfers between devices, shards(): probe_grad = lax.psum(term, ('pos', 'obj'))  157 us
    pallas_call x1, Pallas kernels, pack(): pl.pallas_call(functools.partial(pack_kernel, n_pos), out_shape=(jax.Shap...  130 us
    pallas_call x2, Pallas kernels, compute(): pl.pallas_call(functools.partial(compute_kernel, first_call, last_call, n...  36.3 us
    all_to_all x1, blocking collectives, shards(): lax.all_to_all(slots[k * n_pos:(k + 1) * n_pos], 'pos', 0, 0, tiled=True)  29.8 us
    ppermute x2, waiting for transfers between devices, exchanged(): lax.ppermute(lax.slice_in_dim(block, size - 1, size, axis=dim), axis, for...  23.8 us
  transfers between devices with their start and end apart: 7, of which 4 were waited for; matrix products, arithmetic and copies ran while one was open for 2% of the time, Pallas kernels for 5%

profile of v1, /device:TPU:1, one launch (start us, length us, event | category | flops | bytes accessed | tf_op | source)
XLA Modules:
  0.0 431.3 jit_solution(10508410911899324770)
XLA Ops:
  7.2 130.5 %pack.1 = (bf16[32,256,256]{2,1,0:T(8,128)(2,1)}, s32[32,2]{1,0:T(8,128)}) custom-call(s32[16]{0:T(128)} %owner.1, s32[16]{0:T(128)} %rows.1, s32[16]{0:T(128)} %cols.1, bf16[16,256,256]{2,1,0:T(8,128)(2,1)} %amps.1), custom_call_target="tpu_custom_call" | custom-call | tf_op jit(solution)/shard_map/pack/pallas_call | solution.py:73
  137.7 1.5 copy.14
  139.2 7.6 %all-to-all-start = ((s32[2,16,2]{0,2,1:T(2,128)}), s32[2,16,2]{0,2,1:T(2,128)S(1)}, u32[]{:S(2)}, u32[]{:S(2)}) async-start(s32[2,16,2]{0,2,1:T(2,128)} %copy.14), calls=%async_computation | async-start | bytes 32768 | tf_op jit(solution)/shard_map/all_to_all | solution.py:285
  146.8 3.9 fusion.6
  150.7 2.5 all-to-all-done
  153.2 29.8 %all_to_all.15.amp = bf16[16,256,256]{2,1,0:T(8,128)(2,1)} all-to-all(bf16[16,256,256]{2,1,0:T(8,128)(2,1)S(1)} %get-tuple-element.14), channel_id=1, replica_groups=mesh['pos'=16,'obj'=8] {'pos'}, dimensions={0} | all-to-all | bytes 4194304 | tf_op jit(solution)/shard_map/all_to_all | solution.py:282
  183.0 0.0 copy-start
  183.0 4.9 %all-to-all-start.1 = ((bf16[16,256,256]{2,1,0:T(8,128)(2,1)}), bf16[16,256,256]{2,1,0:T(8,128)(2,1)}, u32[]{:S(2)}, u32[]{:S(2)}) async-start(bf16[16,256,256]{2,1,0:T(8,128)(2,1)} %get-tuple-element.15), calls=%async_computation.1 | async-start | bytes 4194304 | tf_op jit(solution)/shard_map/all_to_all | solution.py:282
  188.0 0.0 all-reduce.2.cloned.1.call-start
  188.0 0.0 copy-done
  188.0 1.0 fusion.8
  189.0 1.3 collective-permute-start.2
  190.3 3.5 collective-permute-start.3
  193.8 5.3 %collective-permute-start = (f32[2,1,384]{2,1,0:T(1,128)S(1)}, f32[2,1,384]{2,1,0:T(1,128)S(1)}, u32[]{:S(2)}, u32[]{:S(2)}) collective-permute-start(f32[2,1,384]{2,1,0:T(1,128)S(1)} %get-tuple-element.16), channel_id=1, source_target_pairs={{0,1},{1,2},{2,3},{3,4},{4,5},{5,6},{6,7},{7,0},{8,9},{9,10},{10,1... | collective-permute-start | bytes 9224 | tf_op jit(solution)/shard_map/ppermute | solution.py:270
  199.1 0.0 collective-permute-start.1
  199.1 0.1 fusion.9
  199.2 0.1 copy.16
  199.2 0.7 copy.17.meta
  199.9 0.1 copy.15
  200.0 0.7 copy.18.meta
  200.7 0.0 collective-permute-done
  200.7 1.8 collective-permute-done.1
  202.5 23.8 %collective-permute-done.2 = f32[2,512,1]{2,1,0:T(8,128)S(1)} collective-permute-done((f32[2,512,1]{2,1,0:T(8,128)}, f32[2,512,1]{2,1,0:T(8,128)S(1)}, u32[]{:S(2)}, u32[]{:S(2)}) %collective-permute-start.2) | collective-permute-done | bytes 4128 | tf_op jit(solution)/shard_map/ppermute | solution.py:270
  226.2 0.0 collective-permute-done.3
  226.2 2.2 fusion.2.base
  228.4 0.6 broadcast_in_dim.3.acc_in.term_in.base
  229.0 19.8 %positions.2 = (f32[2,3,512,128]{3,2,1,0:T(8,128)}, f32[2,256,256]{2,1,0:T(8,128)}) custom-call(s32[16,2]{1,0:T(8,128)} %copy.17.meta, f32[2,512,384]{2,1,0:T(8,128)} %obj.3, f32[2,256,256]{2,1,0:T(8,128)} %probe.3, bf16[512,512]{1,0:T(8,128)(2,1)} %constant.23.left, bf16[512,512]{1,0:T(8,128)(2,1)} %constant.26.right, ...), custom_call_target="tpu_custom_call" | custom-call | flops 8589934592 | bytes 16777216 | tf_op jit(solution)/shard_map/positions/pallas_call | solution.py:228
  248.8 0.0 all-to-all-done.1.amp
  248.8 0.0 copy-start.1
  248.8 16.5 %positions.3 = (f32[2,512,384]{2,1,0:T(8,128)}, f32[2,256,256]{2,1,0:T(8,128)}) custom-call(s32[16,2]{1,0:T(8,128)} %copy.18.meta, f32[2,512,384]{2,1,0:T(8,128)} %obj.3, f32[2,256,256]{2,1,0:T(8,128)} %probe.3, bf16[512,512]{1,0:T(8,128)(2,1)} %constant.23.left, bf16[512,512]{1,0:T(8,128)(2,1)} %constant.26.right, ...), custom_call_target="tpu_custom_call" | custom-call | flops 8589934592 | bytes 16777216 | tf_op jit(solution)/shard_map/positions/pallas_call | solution.py:228
  265.3 0.0 all-reduce.2.cloned.1.call-update
  265.3 157.2 %all-reduce.2.cloned.1.call-done = f32[2,256,256]{2,1,0:T(8,128)} async-done(((f32[2,256,256]{2,1,0:T(8,128)}), f32[2,256,256]{2,1,0:T(8,128)}) %all-reduce.2.cloned.1.call-update) | async-done | bytes 524304 | tf_op jit(solution)/shard_map/psum | solution.py:297
  422.6 0.0 copy-done.1
  422.6 1.9 multiply_subtract_fusion
  (1 shorter events, 0.0 us)
Async XLA Ops:
  139.2 14.0 %all-to-all-start = ((s32[2,16,2]{0,2,1:T(2,128)}), s32[2,16,2]{0,2,1:T(2,128)S(1)}, u32[]{:S(2)}, u32[]{:S(2)}) async-start(s32[2,16,2]{0,2,1:T(2,128)} %copy.14), calls=%async_computation | async-start | bytes 32768 | tf_op jit(solution)/shard_map/all_to_all | solution.py:285
  183.0 5.0 %copy-start = (f32[2,512,384]{2,1,0:T(8,128)S(1)}, f32[2,512,384]{2,1,0:T(8,128)}, u32[]{:S(2)}) copy-start(f32[2,512,384]{2,1,0:T(8,128)} %obj.3) | copy-start | bytes 4718596
  183.0 65.8 %all-to-all-start.1 = ((bf16[16,256,256]{2,1,0:T(8,128)(2,1)}), bf16[16,256,256]{2,1,0:T(8,128)(2,1)}, u32[]{:S(2)}, u32[]{:S(2)}) async-start(bf16[16,256,256]{2,1,0:T(8,128)(2,1)} %get-tuple-element.15), calls=%async_computation.1 | async-start | bytes 4194304 | tf_op jit(solution)/shard_map/all_to_all | solution.py:282
  188.0 234.6 %all-reduce.2.cloned.1.call-start = ((), (), s32[]{:S(2)}) async-start(), calls=%async_computation.3 | async-start | bytes 1048576 | tf_op jit(solution)/shard_map/psum | solution.py:297
  189.0 37.2 %collective-permute-start.2 = (f32[2,512,1]{2,1,0:T(8,128)}, f32[2,512,1]{2,1,0:T(8,128)S(1)}, u32[]{:S(2)}, u32[]{:S(2)}) collective-permute-start(f32[2,512,1]{2,1,0:T(8,128)} %get-tuple-element.18), channel_id=1, source_target_pairs={{0,8},{8,16},{16,24},{24,32},{32,40},{40,48},{48,56},{56,64},{64,7... | collective-permute-start | bytes 12296 | tf_op jit(solution)/shard_map/ppermute | solution.py:270
  190.3 35.9 %collective-permute-start.3 = (f32[2,512,1]{2,1,0:T(8,128)S(1)}, f32[2,512,1]{2,1,0:T(8,128)S(1)}, u32[]{:S(2)}, u32[]{:S(2)}) collective-permute-start(f32[2,512,1]{2,1,0:T(8,128)S(1)} %get-tuple-element.19), channel_id=1, source_target_pairs={{8,0},{16,8},{24,16},{32,24},{40,32},{48,40},{56,48},{64,56},{72,6... | collective-permute-start | bytes 12296 | tf_op jit(solution)/shard_map/ppermute | solution.py:271
  193.8 6.9 %collective-permute-start = (f32[2,1,384]{2,1,0:T(1,128)S(1)}, f32[2,1,384]{2,1,0:T(1,128)S(1)}, u32[]{:S(2)}, u32[]{:S(2)}) collective-permute-start(f32[2,1,384]{2,1,0:T(1,128)S(1)} %get-tuple-element.16), channel_id=1, source_target_pairs={{0,1},{1,2},{2,3},{3,4},{4,5},{5,6},{6,7},{7,0},{8,9},{9,10},{10,1... | collective-permute-start | bytes 9224 | tf_op jit(solution)/shard_map/ppermute | solution.py:270
  199.1 3.4 collective-permute-start.1
  248.8 173.7 %copy-start.1 = (f32[2,256,256]{2,1,0:T(8,128)S(1)}, f32[2,256,256]{2,1,0:T(8,128)}, u32[]{:S(2)}) copy-start(f32[2,256,256]{2,1,0:T(8,128)} %probe.3) | copy-start | bytes 1572868
Sparse Core Ops, SparseCore 0:
  265.4 157.0 all-reduce.1

commit v2 on v1

--- a/solution.py
+++ b/solution.py
@@ -33,7 +33,7 @@
     return left, jnp.concatenate([top, bottom], axis=0)
 
 
-def pack_kernel(n_pos, owner, rows, cols, amps, slots, meta, source, count, sems):
+def pack_kernel(n_pos, owner, rows, cols, amps, slots, meta, source, count):
     total = n_pos * CAPACITY
     n_dev = owner.shape[0]
 
@@ -59,30 +59,26 @@
 
     @pl.loop(0, total)
     def _(i):
-        pltpu.make_async_copy(amps.at[source[i]], slots.at[i], sems.at[i]).start()
-
-    @pl.loop(0, total)
-    def _(i):
-        pltpu.make_async_copy(amps.at[source[i]], slots.at[i], sems.at[i]).wait()
+        slots[i] = amps[source[i]]
 
 
 def pack(owner, rows, cols, amps, n_pos):
     total = n_pos * CAPACITY
     smem = pl.BlockSpec(memory_space=pltpu.SMEM)
-    hbm = pl.BlockSpec(memory_space=pl.ANY)
+    vmem = pl.BlockSpec(memory_space=pltpu.VMEM)
     return pl.pallas_call(
         functools.partial(pack_kernel, n_pos),
         out_shape=(
             jax.ShapeDtypeStruct((total, SIZE, SIZE), BF16),
             jax.ShapeDtypeStruct((total, 2), jnp.int32),
         ),
-        in_specs=[smem, smem, smem, hbm],
-        out_specs=(hbm, smem),
+        in_specs=[smem, smem, smem, vmem],
+        out_specs=(vmem, smem),
         scratch_shapes=[
             pltpu.SMEM((total,), jnp.int32),
             pltpu.SMEM((n_pos,), jnp.int32),
-            pltpu.SemaphoreType.DMA((total,)),
         ],
+        compiler_params=pltpu.CompilerParams(vmem_limit_bytes=24 << 20),
         name="pack",
     )(owner, rows, cols, amps)
 
@@ -262,6 +258,114 @@
     )(meta, obj, probe, left, right, amp, acc_in, term_in, base)
 
 
+MESH = pl.DeviceIdType.MESH
+
+
+def sum_kernel(n_pos, n_obj, scale, term, probe, out, tiles, got_obj, part, got_pos, done, send, recv):
+    me_p = lax.axis_index("pos")
+    me_o = lax.axis_index("obj")
+    peer_o = [lax.rem(me_o + d, n_obj) for d in range(1, n_obj)]
+    peer_p = [lax.rem(me_p + d, n_pos) for d in range(1, n_pos)]
+
+    barrier = pltpu.get_barrier_semaphore()
+    for o in peer_o:
+        pl.semaphore_signal(barrier, inc=1, device_id=(me_p, o), device_id_type=MESH)
+    for p in peer_p:
+        pl.semaphore_signal(barrier, inc=1, device_id=(p, me_o), device_id_type=MESH)
+    pl.semaphore_wait(barrier, n_obj + n_pos - 2)
+
+    for part_i in range(2):
+        for i in range(SIZE // 8):
+            for k in range(2):
+                tiles[(part_i * (SIZE // 8) + i) * 2 + k] = term[
+                    part_i, 8 * i : 8 * i + 8, k * LANES : (k + 1) * LANES
+                ]
+
+    def over_obj(base, source_of, target_of):
+        return [
+            pltpu.make_async_remote_copy(
+                src_ref=source_of(d, o), dst_ref=target_of(d, o),
+                send_sem=send.at[base + d], recv_sem=recv.at[base + d],
+                device_id=(me_p, o), device_id_type=MESH,
+            )
+            for d, o in enumerate(peer_o)
+        ]
+
+    def over_pos(base, source_of, target_of):
+        return [
+            pltpu.make_async_remote_copy(
+                src_ref=source_of(d, p), dst_ref=target_of(d, p),
+                send_sem=send.at[base + d], recv_sem=recv.at[base + d],
+                device_id=(p, me_o), device_id_type=MESH,
+            )
+            for d, p in enumerate(peer_p)
+        ]
+
+    step = n_obj - 1 + n_pos - 1
+    copies = over_obj(0, lambda d, o: tiles.at[pl.ds(o * n_pos, n_pos)], lambda d, o: got_obj.at[d])
+    for c in copies:
+        c.start()
+    for c in copies:
+        c.wait_recv()
+    total = tiles[pl.ds(me_o * n_pos, n_pos)]
+    for d in range(n_obj - 1):
+        total += got_obj[d]
+    part[...] = total
+    second = over_pos(n_obj - 1, lambda d, p: part.at[p], lambda d, p: got_pos.at[d])
+    for c in second:
+        c.start()
+    for c in second:
+        c.wait_recv()
+    total = part[me_p]
+    for d in range(n_pos - 1):
+        total += got_pos[d]
+    mine = me_o * n_pos + me_p
+    done[mine] = total
+    third = over_pos(step, lambda d, p: done.at[mine], lambda d, p: done.at[mine])
+    for c in third:
+        c.start()
+    for c in third:
+        c.wait_recv()
+    block = pl.ds(me_o * n_pos, n_pos)
+    fourth = over_obj(step + n_pos - 1, lambda d, o: done.at[block], lambda d, o: done.at[block])
+    for c in fourth:
+        c.start()
+    for c in fourth:
+        c.wait_recv()
+    for c in copies + second + third + fourth:
+        c.wait_send()
+    for part_i in range(2):
+        for i in range(SIZE // 8):
+            for k in range(2):
+                rows, cols = slice(8 * i, 8 * i + 8), slice(k * LANES, (k + 1) * LANES)
+                out[part_i, rows, cols] = probe[part_i, rows, cols] - scale * done[
+                    (part_i * (SIZE // 8) + i) * 2 + k
+                ]
+
+
+def summed(term, probe, n_pos, n_obj, scale):
+    count = 2 * (n_pos + n_obj - 2)
+    vmem = pl.BlockSpec(memory_space=pltpu.VMEM)
+    tiles = n_pos * n_obj
+    return pl.pallas_call(
+        functools.partial(sum_kernel, n_pos, n_obj, scale),
+        out_shape=jax.ShapeDtypeStruct(probe.shape, F32),
+        in_specs=[vmem, vmem],
+        out_specs=vmem,
+        scratch_shapes=[
+            pltpu.VMEM((tiles, 8, LANES), F32),
+            pltpu.VMEM((n_obj - 1, n_pos, 8, LANES), F32),
+            pltpu.VMEM((n_pos, 8, LANES), F32),
+            pltpu.VMEM((n_pos - 1, 8, LANES), F32),
+            pltpu.VMEM((tiles, 8, LANES), F32),
+            pltpu.SemaphoreType.DMA((count,)),
+            pltpu.SemaphoreType.DMA((count,)),
+        ],
+        compiler_params=pltpu.CompilerParams(collective_id=1, has_side_effects=True),
+        name="probe_sum",
+    )(term, probe)
+
+
 def exchanged(block, axis, dim):
     count = lax.axis_size(axis)
     forward = [(i, (i + 1) % count) for i in range(count)]
@@ -294,9 +398,8 @@
     new_object, term = compute(
         False, True, corners[1], object_field, probe, left, right, arrived[1], acc, term, base
     )
-    probe_grad = lax.psum(term, ("pos", "obj"))
-    n_total = pos_dev * n_pos * n_obj
-    return new_object, probe - probe_grad * (1.0 / math.sqrt(n_total))
+    scale = 1.0 / math.sqrt(pos_dev * n_pos * n_obj)
+    return new_object, summed(term, probe, n_pos, n_obj, scale)
 
 
 def solution(mesh):

time: 432 us -> 180 us (0.42)
  waiting for transfers between devices: 185 us -> 28.1 us
  Pallas kernels: 167 us -> 80.7 us
  between operations: 14.1 us -> 0.7 us
  local copies, waits for them, and re-layouts: 8.69 us -> 15.3 us
    psum x1 -> x0, waiting for transfers between devices: 157 us -> none  [shards(): probe_grad = lax.psum(term, ('pos', 'obj'))]
    pallas_call x1, Pallas kernels: 130 us -> 2.41 us  [pack(): pl.pallas_call(functools.partial(pack_kernel, n_pos), out_shape=(jax.Shap...]
    pallas_call x0 -> x1, Pallas kernels: none -> 45.3 us  [summed(): pl.pallas_call(functools.partial(sum_kernel, n_pos, n_obj, scale), out_sh...]
    unnamed x4 -> x13, local copies, waits for them, and re-layouts: 0.01 us -> 7.36 us
  transfers between devices with their start and end apart: 7 -> 6, of which waited for: 4 -> 3; matrix products, arithmetic and copies ran while one was open for 2% -> 5% of each run, Pallas kernels for 5% -> 13%
where the time goes in v2:
time: 180 us; the launch traced here: 179 us
  Pallas kernels  80.7 us (45%)
  blocking collectives  29.8 us (17%)
  waiting for transfers between devices  28.1 us (16%)
  starting transfers between devices  22.6 us (13%)
  local copies, waits for them, and re-layouts  15.3 us (8%)
  other arithmetic  2.16 us (1%)
    pallas_call x1, Pallas kernels, summed(): pl.pallas_call(functools.partial(sum_kernel, n_pos, n_obj, scale), out_sh...  45.3 us
    pallas_call x2, Pallas kernels, compute(): pl.pallas_call(functools.partial(compute_kernel, first_call, last_call, n...  33.1 us
    all_to_all x1, blocking collectives, shards(): lax.all_to_all(slots[k * n_pos:(k + 1) * n_pos], 'pos', 0, 0, tiled=True)  29.8 us
    ppermute x2, waiting for transfers between devices, exchanged(): lax.ppermute(lax.slice_in_dim(block, size - 1, size, axis=dim), axis, for...  23.8 us
    all_to_all x1, starting transfers between devices, shards(): lax.all_to_all(meta.reshape(CAPACITY, n_pos, 2), 'pos', 1, 1, tiled=True)  7.58 us
    unnamed x13, local copies, waits for them, and re-layouts  7.36 us
    ppermute x2, starting transfers between devices, exchanged(): lax.ppermute(lax.slice_in_dim(block, size - 1, size, axis=dim), axis, for...  6.57 us
    all_to_all x1, starting transfers between devices, shards(): lax.all_to_all(slots[k * n_pos:(k + 1) * n_pos], 'pos', 0, 0, tiled=True)  4.92 us
  transfers between devices with their start and end apart: 6, of which 3 were waited for; matrix products, arithmetic and copies ran while one was open for 5% of the time, Pallas kernels for 13%

profile of v2, /device:TPU:1, one launch (start us, length us, event | category | flops | bytes accessed | tf_op | source)
XLA Modules:
  0.0 179.4 jit_solution(15223587709356105520)
XLA Ops:
  0.6 0.0 copy-start.1
  0.6 1.6 copy-done.1
  2.2 0.0 copy-start.2
  2.2 0.7 copy-done.2
  2.9 0.0 copy-start.3
  2.9 0.7 copy-done.3
  3.5 0.0 copy-start.4
  3.5 0.7 copy-done.4
  4.2 2.4 %pack.1 = (bf16[32,256,256]{2,1,0:T(8,128)(2,1)S(1)}, s32[32,2]{1,0:T(8,128)S(1)}) custom-call(s32[16]{0:T(128)S(1)} %copy-done.2, s32[16]{0:T(128)S(1)} %copy-done.3, s32[16]{0:T(128)S(1)} %copy-done.4, bf16[16,256,256]{2,1,0:T(8,128)(2,1)S(1)} %copy-done.1), custom_call_target="tpu_custom_call" | custom-call | tf_op jit(solution)/shard_map/pack/pallas_call | solution.py:69
  6.6 0.0 copy-start
  6.6 1.9 %copy-done = bf16[32,256,256]{2,1,0:T(8,128)(2,1)} copy-done((bf16[32,256,256]{2,1,0:T(8,128)(2,1)}, bf16[32,256,256]{2,1,0:T(8,128)(2,1)S(1)}, u32[]{:S(2)}) %copy-start) | copy-done | bytes 4194328
  8.6 0.8 copy.14
  9.4 7.6 %all-to-all-start = ((s32[2,16,2]{0,2,1:T(2,128)}), s32[2,16,2]{0,2,1:T(2,128)S(1)}, u32[]{:S(2)}, u32[]{:S(2)}) async-start(s32[2,16,2]{0,2,1:T(2,128)} %copy.14), calls=%async_computation | async-start | bytes 32768 | tf_op jit(solution)/shard_map/all_to_all | solution.py:389
  17.0 3.9 %fusion.6 = (bf16[16,256,256]{2,1,0:T(8,128)(2,1)S(1)}, bf16[16,256,256]{2,1,0:T(8,128)(2,1)}) fusion(bf16[32,256,256]{2,1,0:T(8,128)(2,1)} %copy-done), kind=kLoop, calls=%fused_computation.10 | loop fusion | bytes 8388608 | tf_op jit(solution)/shard_map/slice | solution.py:386
  20.9 2.5 %all-to-all-done = s32[2,16,2]{0,2,1:T(2,128)S(1)} async-done(((s32[2,16,2]{0,2,1:T(2,128)}), s32[2,16,2]{0,2,1:T(2,128)S(1)}, u32[]{:S(2)}, u32[]{:S(2)}) %all-to-all-start) | async-done | bytes 288 | tf_op jit(solution)/shard_map/all_to_all | solution.py:389
  23.4 29.8 %all_to_all.15.amp = bf16[16,256,256]{2,1,0:T(8,128)(2,1)} all-to-all(bf16[16,256,256]{2,1,0:T(8,128)(2,1)S(1)} %get-tuple-element.14), channel_id=1, replica_groups=mesh['pos'=16,'obj'=8] {'pos'}, dimensions={0} | all-to-all | bytes 4194304 | tf_op jit(solution)/shard_map/all_to_all | solution.py:386
  53.2 0.0 copy-start.5
  53.2 4.9 %all-to-all-start.1 = ((bf16[16,256,256]{2,1,0:T(8,128)(2,1)}), bf16[16,256,256]{2,1,0:T(8,128)(2,1)}, u32[]{:S(2)}, u32[]{:S(2)}) async-start(bf16[16,256,256]{2,1,0:T(8,128)(2,1)} %get-tuple-element.15), calls=%async_computation.1 | async-start | bytes 4194304 | tf_op jit(solution)/shard_map/all_to_all | solution.py:386
  58.1 0.0 copy-done.5
  58.2 1.0 fusion.8
  59.1 1.3 collective-permute-start.2
  60.5 3.5 %collective-permute-start.3 = (f32[2,512,1]{2,1,0:T(8,128)S(1)}, f32[2,512,1]{2,1,0:T(8,128)S(1)}, u32[]{:S(2)}, u32[]{:S(2)}) collective-permute-start(f32[2,512,1]{2,1,0:T(8,128)S(1)} %get-tuple-element.19), channel_id=1, source_target_pairs={{8,0},{16,8},{24,16},{32,24},{40,32},{48,40},{56,48},{64,56},{72,6... | collective-permute-start | bytes 12296 | tf_op jit(solution)/shard_map/ppermute | solution.py:375
  63.9 5.3 %collective-permute-start = (f32[2,1,384]{2,1,0:T(1,128)S(1)}, f32[2,1,384]{2,1,0:T(1,128)S(1)}, u32[]{:S(2)}, u32[]{:S(2)}) collective-permute-start(f32[2,1,384]{2,1,0:T(1,128)S(1)} %get-tuple-element.16), channel_id=1, source_target_pairs={{0,1},{1,2},{2,3},{3,4},{4,5},{5,6},{6,7},{7,0},{8,9},{9,10},{10,1... | collective-permute-start | bytes 9224 | tf_op jit(solution)/shard_map/ppermute | solution.py:374
  69.2 0.0 collective-permute-start.1
  69.2 0.1 fusion.9
  69.3 0.1 copy.16
  69.4 0.7 copy.17.meta
  70.1 0.1 copy.15
  70.2 0.7 copy.18.meta
  70.8 0.0 collective-permute-done
  70.8 1.8 collective-permute-done.1
  72.6 23.8 %collective-permute-done.2 = f32[2,512,1]{2,1,0:T(8,128)S(1)} collective-permute-done((f32[2,512,1]{2,1,0:T(8,128)}, f32[2,512,1]{2,1,0:T(8,128)S(1)}, u32[]{:S(2)}, u32[]{:S(2)}) %collective-permute-start.2) | collective-permute-done | bytes 4128 | tf_op jit(solution)/shard_map/ppermute | solution.py:374
  96.4 0.0 collective-permute-done.3
  96.4 2.2 %fusion.2.base = f32[2,512,384]{2,1,0:T(8,128)} fusion(f32[2,512,384]{2,1,0:T(8,128)S(1)} %copy-done.5, f32[2,512,1]{2,1,0:T(8,128)S(1)} %collective-permute-done.3, f32[2,512,1]{2,1,0:T(8,128)S(1)} %collective-permute-done.2, f32[2,1,384]{2,1,0:T(1,128)S(1)} %collective-permute-done.1, f32[2,1,384]{2,1,0:T(1,128)S(1)} %collective-permute-done), kind=kLoop, calls=%fused_computation.3 | loop fusion | flops 4325376 | bytes 3160064 | tf_op jit(solution)/shard_map/sub | solution.py:393
  98.6 0.6 broadcast_in_dim.3.acc_in.term_in.base
  99.2 22.7 %positions.2 = (f32[2,3,512,128]{3,2,1,0:T(8,128)}, f32[2,256,256]{2,1,0:T(8,128)}) custom-call(s32[16,2]{1,0:T(8,128)} %copy.17.meta, f32[2,512,384]{2,1,0:T(8,128)} %obj.3, f32[2,256,256]{2,1,0:T(8,128)} %probe.5, bf16[512,512]{1,0:T(8,128)(2,1)} %constant.21.left, bf16[512,512]{1,0:T(8,128)(2,1)} %constant.24.right, ...), custom_call_target="tpu_custom_call" | custom-call | flops 8589934592 | bytes 16777216 | tf_op jit(solution)/shard_map/positions/pallas_call | solution.py:224
  121.9 0.0 all-to-all-done.1.amp
  121.9 10.3 %positions.3 = (f32[2,512,384]{2,1,0:T(8,128)}, f32[2,256,256]{2,1,0:T(8,128)}) custom-call(s32[16,2]{1,0:T(8,128)} %copy.18.meta, f32[2,512,384]{2,1,0:T(8,128)} %obj.3, f32[2,256,256]{2,1,0:T(8,128)} %probe.5, bf16[512,512]{1,0:T(8,128)(2,1)} %constant.21.left, bf16[512,512]{1,0:T(8,128)(2,1)} %constant.24.right, ...), custom_call_target="tpu_custom_call" | custom-call | flops 8589934592 | bytes 16777216 | tf_op jit(solution)/shard_map/positions/pallas_call | solution.py:224
  132.3 45.3 %probe_sum.1 = f32[2,256,256]{2,1,0:T(8,128)} custom-call(f32[2,256,256]{2,1,0:T(8,128)} %get-tuple-element.13.term, f32[2,256,256]{2,1,0:T(8,128)} %probe.5), custom_call_target="tpu_custom_call" | custom-call | tf_op jit(solution)/shard_map/probe_sum/pallas_call | solution.py:350
  177.5 1.9 %copy.22 = f32[2,256,256]{2,1,0:T(8,128)} copy(f32[2,256,256]{2,1,0:T(8,128)} %probe_sum.1) | data formatting | bytes 1048576
  (1 shorter events, 0.0 us)
Async XLA Ops:
  0.6 1.6 copy-start.1
  2.2 0.7 copy-start.2
  2.9 0.7 copy-start.3
  3.5 0.7 copy-start.4
  6.6 1.9 %copy-start = (bf16[32,256,256]{2,1,0:T(8,128)(2,1)}, bf16[32,256,256]{2,1,0:T(8,128)(2,1)S(1)}, u32[]{:S(2)}) copy-start(bf16[32,256,256]{2,1,0:T(8,128)(2,1)S(1)} %get-tuple-element.9) | copy-start | bytes 12582916
  9.4 14.0 %all-to-all-start = ((s32[2,16,2]{0,2,1:T(2,128)}), s32[2,16,2]{0,2,1:T(2,128)S(1)}, u32[]{:S(2)}, u32[]{:S(2)}) async-start(s32[2,16,2]{0,2,1:T(2,128)} %copy.14), calls=%async_computation | async-start | bytes 32768 | tf_op jit(solution)/shard_map/all_to_all | solution.py:389
  53.2 4.9 %copy-start.5 = (f32[2,512,384]{2,1,0:T(8,128)S(1)}, f32[2,512,384]{2,1,0:T(8,128)}, u32[]{:S(2)}) copy-start(f32[2,512,384]{2,1,0:T(8,128)} %obj.3) | copy-start | bytes 4718596
  53.2 68.7 %all-to-all-start.1 = ((bf16[16,256,256]{2,1,0:T(8,128)(2,1)}), bf16[16,256,256]{2,1,0:T(8,128)(2,1)}, u32[]{:S(2)}, u32[]{:S(2)}) async-start(bf16[16,256,256]{2,1,0:T(8,128)(2,1)} %get-tuple-element.15), calls=%async_computation.1 | async-start | bytes 4194304 | tf_op jit(solution)/shard_map/all_to_all | solution.py:386
  59.1 37.3 %collective-permute-start.2 = (f32[2,512,1]{2,1,0:T(8,128)}, f32[2,512,1]{2,1,0:T(8,128)S(1)}, u32[]{:S(2)}, u32[]{:S(2)}) collective-permute-start(f32[2,512,1]{2,1,0:T(8,128)} %get-tuple-element.18), channel_id=1, source_target_pairs={{0,8},{8,16},{16,24},{24,32},{32,40},{40,48},{48,56},{56,64},{64,7... | collective-permute-start | bytes 12296 | tf_op jit(solution)/shard_map/ppermute | solution.py:374
  60.5 36.0 %collective-permute-start.3 = (f32[2,512,1]{2,1,0:T(8,128)S(1)}, f32[2,512,1]{2,1,0:T(8,128)S(1)}, u32[]{:S(2)}, u32[]{:S(2)}) collective-permute-start(f32[2,512,1]{2,1,0:T(8,128)S(1)} %get-tuple-element.19), channel_id=1, source_target_pairs={{8,0},{16,8},{24,16},{32,24},{40,32},{48,40},{56,48},{64,56},{72,6... | collective-permute-start | bytes 12296 | tf_op jit(solution)/shard_map/ppermute | solution.py:375
  63.9 6.9 %collective-permute-start = (f32[2,1,384]{2,1,0:T(1,128)S(1)}, f32[2,1,384]{2,1,0:T(1,128)S(1)}, u32[]{:S(2)}, u32[]{:S(2)}) collective-permute-start(f32[2,1,384]{2,1,0:T(1,128)S(1)} %get-tuple-element.16), channel_id=1, source_target_pairs={{0,1},{1,2},{2,3},{3,4},{4,5},{5,6},{6,7},{7,0},{8,9},{9,10},{10,1... | collective-permute-start | bytes 9224 | tf_op jit(solution)/shard_map/ppermute | solution.py:374
  69.2 3.4 %collective-permute-start.1 = (f32[2,1,384]{2,1,0:T(1,128)S(1)}, f32[2,1,384]{2,1,0:T(1,128)S(1)}, u32[]{:S(2)}, u32[]{:S(2)}) collective-permute-start(f32[2,1,384]{2,1,0:T(1,128)S(1)} %get-tuple-element.17), channel_id=1, source_target_pairs={{1,0},{2,1},{3,2},{4,3},{5,4},{6,5},{7,6},{0,7},{9,8},{10,9},{11,1... | collective-permute-start | bytes 9224 | tf_op jit(solution)/shard_map/ppermute | solution.py:375

commit v3 on v2

v3 whole, which is shorter than its diff:
```python
import functools
import math

import jax
import jax.numpy as jnp
import numpy as np
from jax import lax
from jax.experimental import pallas as pl
from jax.experimental.pallas import tpu as pltpu
from jax.sharding import PartitionSpec as P

SIZE = 256
CAPACITY = 2
LANES = 128
F32 = jnp.float32
BF16 = jnp.bfloat16


def dft_blocks():
    index = np.arange(SIZE, dtype=np.int64)
    product = (index[:, None] * index[None, :]) % SIZE
    angle = product.astype(np.float32) * np.float32(2.0 * math.pi / SIZE)
    scale = 1.0 / math.sqrt(SIZE)
    real = (np.cos(angle.astype(np.float64)) * scale).astype(np.float32)
    imag = (-np.sin(angle.astype(np.float64)) * scale).astype(np.float32)
    real = jnp.asarray(real).astype(BF16)
    imag = jnp.asarray(imag).astype(BF16)
    top = jnp.concatenate([real, -imag], axis=1)
    bottom = jnp.concatenate([imag, real], axis=1)
    left = jnp.concatenate([top, bottom], axis=0)
    top = jnp.concatenate([real, imag], axis=1)
    bottom = jnp.concatenate([-imag, real], axis=1)
    return left, jnp.concatenate([top, bottom], axis=0)


STRIP = 32


def extract(meta_row, meta_col, tile, probe, window, psi, j):
    lane = lax.broadcasted_iota(jnp.int32, (STRIP, LANES), 1)
    first = lane < LANES - meta_col
    shift = lax.rem(LANES - meta_col, LANES)
    for s in range(0, SIZE, STRIP):
        parts = []
        for p in range(2):
            t = [
                pltpu.roll(tile[p, k, pl.ds(meta_row + s, STRIP), :], shift, 1)
                for k in range(3)
            ]
            parts.append([jnp.where(first, t[k], t[k + 1]) for k in range(2)])
        for k in range(2):
            cols = slice(k * LANES, (k + 1) * LANES)
            x_re, x_im = parts[0][k], parts[1][k]
            window[j, 0, s : s + STRIP, cols] = x_re
            window[j, 1, s : s + STRIP, cols] = x_im
            p_re = probe[0, s : s + STRIP, cols]
            p_im = probe[1, s : s + STRIP, cols]
            out = slice(j * SIZE + k * LANES, j * SIZE + (k + 1) * LANES)
            psi[s : s + STRIP, out] = (p_re * x_re - p_im * x_im).astype(BF16)
            psi[SIZE + s : SIZE + s + STRIP, out] = (p_re * x_im + p_im * x_re).astype(BF16)


def turn(value, out):
    for j in range(2):
        for part in range(2):
            out[j * SIZE : (j + 1) * SIZE, part * SIZE : (part + 1) * SIZE] = value[
                part * SIZE : (part + 1) * SIZE, j * SIZE : (j + 1) * SIZE
            ].astype(BF16)


def modulus(wave, amp, diff, j):
    for s in range(0, SIZE, STRIP):
        rows = slice(j * SIZE + s, j * SIZE + s + STRIP)
        w_re = wave[rows, 0:SIZE]
        w_im = wave[rows, SIZE : 2 * SIZE]
        a = amp[j, s : s + STRIP, :].astype(F32)
        power = w_re * w_re + w_im * w_im
        factor = 1.0 - a * lax.rsqrt(jnp.maximum(power, 0.25))
        cols = slice(j * SIZE, (j + 1) * SIZE)
        diff[s : s + STRIP, cols] = (w_re * factor).astype(BF16)
        diff[SIZE + s : SIZE + s + STRIP, cols] = (w_im * factor).astype(BF16)


def gradients(meta_col, chi, probe, window, spread, term, j):
    lane = lax.broadcasted_iota(jnp.int32, (STRIP, LANES), 1)
    later = lane >= meta_col
    shift = lax.rem(meta_col, LANES)
    zero = jnp.zeros((STRIP, LANES), F32)
    for s in range(0, SIZE, STRIP):
        rows = slice(j * SIZE + s, j * SIZE + s + STRIP)
        turned = [[], []]
        for k in range(2):
            cols = slice(k * LANES, (k + 1) * LANES)
            c_re = chi[rows, k * LANES : (k + 1) * LANES]
            c_im = chi[rows, SIZE + k * LANES : SIZE + (k + 1) * LANES]
            x_re = window[j, 0, s : s + STRIP, cols]
            x_im = window[j, 1, s : s + STRIP, cols]
            term[0, s : s + STRIP, cols] += x_re * c_re + x_im * c_im
            term[1, s : s + STRIP, cols] += x_re * c_im - x_im * c_re
            p_re = probe[0, s : s + STRIP, cols]
            p_im = probe[1, s : s + STRIP, cols]
            g_re = (p_re * c_re + p_im * c_im).astype(BF16).astype(F32)
            g_im = (p_re * c_im - p_im * c_re).astype(BF16).astype(F32)
            turned[0].append(pltpu.roll(g_re, shift, 1))
            turned[1].append(pltpu.roll(g_im, shift, 1))
        here = slice(SIZE + s, SIZE + s + STRIP)
        for p in range(2):
            low, high = turned[p]
            spread[j, p, 0, here, :] = jnp.where(later, low, zero)
            spread[j, p, 1, here, :] = jnp.where(later, high, low)
            spread[j, p, 2, here, :] = jnp.where(later, zero, high)


def accumulate(meta_row, spread, acc):
    starts = [SIZE - jnp.bitwise_and(meta_row[j], 2 * SIZE - 1) for j in range(2)]
    for p in range(2):
        for k in range(3):
            for s in range(0, 2 * SIZE, STRIP):
                acc[p, k, s : s + STRIP, :] += (
                    spread[0, p, k, pl.ds(starts[0] + s, STRIP), :]
                    + spread[1, p, k, pl.ds(starts[1] + s, STRIP), :]
                )


MESH = pl.DeviceIdType.MESH


def fused_kernel(
    n_pos, n_obj, scale,
    owner, rows, cols, amps, obj, probe, left, right,
    grad_out, probe_out,
    slots, landed, meta_out, meta_in, meta, tile, window, psi, half, wave, diff, chi, spread, acc,
    term, tiles, got_obj, part, got_pos, done,
    amp_send, amp_recv, meta_send, meta_recv, meta_sem, sum_send, sum_recv,
):
    me_p = lax.axis_index("pos")
    me_o = lax.axis_index("obj")
    side = math.isqrt(n_pos)
    peer_o = [lax.rem(me_o + d, n_obj) for d in range(1, n_obj)]

    def peer_at(s):
        x = lax.rem(me_p // side + s // side, side)
        y = lax.rem(me_p % side + s % side, side)
        return x * side + y

    peer_p = [peer_at(s) for s in range(1, n_pos)]

    barrier = pltpu.get_barrier_semaphore()
    for o in peer_o:
        pl.semaphore_signal(barrier, inc=1, device_id=(me_p, o), device_id_type=MESH)
    for p in peer_p:
        pl.semaphore_signal(barrier, inc=1, device_id=(p, me_o), device_id_type=MESH)
    pl.semaphore_wait(barrier, n_obj + n_pos - 2)

    def amp_copy(s):
        return pltpu.make_async_remote_copy(
            src_ref=slots.at[s], dst_ref=landed.at[s],
            send_sem=amp_send.at[s], recv_sem=amp_recv.at[s],
            device_id=(peer_at(s), me_o), device_id_type=MESH,
        )

    def meta_copy(s):
        return pltpu.make_async_remote_copy(
            src_ref=meta_out.at[s], dst_ref=meta_in.at[s],
            send_sem=meta_send.at[s], recv_sem=meta_recv.at[s],
            device_id=(peer_at(s), me_o), device_id_type=MESH,
        )

    lane = lax.broadcasted_iota(jnp.int32, (8, LANES), 1)

    def found(s):
        target = peer_at(s)
        first = jnp.int32(-1)
        second = jnp.int32(-1)
        for i in reversed(range(amps.shape[0])):
            hit = owner[i] == target
            second = jnp.where(hit, first, second)
            first = jnp.where(hit, i, first)
        return first, second

    def lay_out(s, out, corners):
        picked = found(s)
        values = jnp.zeros((8, LANES), jnp.int32)
        for k in range(CAPACITY):
            i = jnp.maximum(picked[k], 0)
            row = jnp.where(picked[k] < 0, 2 * SIZE, rows[i])
            values = jnp.where(lane == 2 * k, row, values)
            values = jnp.where(lane == 2 * k + 1, cols[i], values)
            out[s, k] = amps[i]
        corners[s] = values

    @pl.loop(1, n_pos)
    def _(s):
        lay_out(s, slots, meta_out)
        meta_copy(s).start()
        amp_copy(s).start()

    lay_out(0, landed, meta_in)
    for p in range(2):
        for k in range(3):
            block = slice(k * LANES, (k + 1) * LANES)
            tile[p, k, 0 : 2 * SIZE, :] = obj[p, :, block].astype(BF16).astype(F32)
            tile[p, k, 2 * SIZE : 3 * SIZE, :] = jnp.zeros((SIZE, LANES), F32)
            for j in range(2):
                spread[j, p, k, 0:SIZE, :] = jnp.zeros((SIZE, LANES), F32)
                spread[j, p, k, 2 * SIZE : 3 * SIZE, :] = jnp.zeros((SIZE, LANES), F32)
    acc[...] = jnp.zeros_like(acc)
    term[...] = jnp.zeros_like(term)

    @pl.loop(1, n_pos)
    def _(s):
        meta_copy(s).wait()

    to_scalars = pltpu.make_async_copy(meta_in, meta, meta_sem)
    to_scalars.start()
    to_scalars.wait()

    @pl.loop(0, n_pos)
    def _(s):
        @pl.when(s > 0)
        def _():
            amp_copy(s).wait()

        row = [meta[s, 0, 2 * j] for j in range(2)]
        col = [meta[s, 0, 2 * j + 1] for j in range(2)]
        amp = landed.at[s]
        for j in range(2):
            extract(row[j], col[j], tile, probe, window, psi, j)
        turn(jnp.dot(left[...], psi[...], preferred_element_type=F32), half)
        wave[...] = jnp.dot(half[...], right[...], preferred_element_type=F32)
        for j in range(2):
            modulus(wave, amp, diff, j)
        turn(jnp.dot(right[...], diff[...], preferred_element_type=F32), half)
        chi[...] = jnp.dot(half[...], left[...], preferred_element_type=F32)
        for j in range(2):
            gradients(col[j], chi, probe, window, spread, term, j)
        accumulate(row, spread, acc)

    for p in range(2):
        for k in range(3):
            grad_out[p, :, k * LANES : (k + 1) * LANES] = acc[p, k]

    for plane in range(2):
        for i in range(SIZE // 8):
            for k in range(2):
                tiles[(plane * (SIZE // 8) + i) * 2 + k] = term[
                    plane, 8 * i : 8 * i + 8, k * LANES : (k + 1) * LANES
                ]

    def over_obj(base, source_of, target_of):
        return [
            pltpu.make_async_remote_copy(
                src_ref=source_of(d, o), dst_ref=target_of(d, o),
                send_sem=sum_send.at[base + d], recv_sem=sum_recv.at[base + d],
                device_id=(me_p, o), device_id_type=MESH,
            )
            for d, o in enumerate(peer_o)
        ]

    def over_pos(base, source_of, target_of):
        return [
            pltpu.make_async_remote_copy(
                src_ref=source_of(d, p), dst_ref=target_of(d, p),
                send_sem=sum_send.at[base + d], recv_sem=sum_recv.at[base + d],
                device_id=(p, me_o), device_id_type=MESH,
            )
            for d, p in enumerate(peer_p)
        ]

    step = n_obj - 1 + n_pos - 1
    copies = over_obj(0, lambda d, o: tiles.at[pl.ds(o * n_pos, n_pos)], lambda d, o: got_obj.at[d])
    for c in copies:
        c.start()
    for c in copies:
        c.wait_recv()
    total = tiles[pl.ds(me_o * n_pos, n_pos)]
    for d in range(n_obj - 1):
        total += got_obj[d]
    part[...] = total
    second = over_pos(n_obj - 1, lambda d, p: part.at[p], lambda d, p: got_pos.at[d])
    for c in second:
        c.start()
    for c in second:
        c.wait_recv()
    total = part[me_p]
    for d in range(n_pos - 1):
        total += got_pos[d]
    mine = me_o * n_pos + me_p
    done[mine] = total
    third = over_pos(step, lambda d, p: done.at[mine], lambda d, p: done.at[mine])
    for c in third:
        c.start()
    for c in third:
        c.wait_recv()
    block = pl.ds(me_o * n_pos, n_pos)
    fourth = over_obj(step + n_pos - 1, lambda d, o: done.at[block], lambda d, o: done.at[block])
    for c in fourth:
        c.start()
    for c in fourth:
        c.wait_recv()
    for c in copies + second + third + fourth:
        c.wait_send()
    for plane in range(2):
        for i in range(SIZE // 8):
            for k in range(2):
                here, block = slice(8 * i, 8 * i + 8), slice(k * LANES, (k + 1) * LANES)
                probe_out[plane, here, block] = probe[plane, here, block] - scale * done[
                    (plane * (SIZE // 8) + i) * 2 + k
                ]


def fused(owner, rows, cols, amps, obj, probe, left, right, n_pos, n_obj, scale):
    smem = pl.BlockSpec(memory_space=pltpu.SMEM)
    vmem = pl.BlockSpec(memory_space=pltpu.VMEM)
    count = 2 * (n_pos + n_obj - 2)
    total = n_pos * n_obj
    double = (2 * SIZE, 2 * SIZE)
    dma = pltpu.SemaphoreType.DMA
    return pl.pallas_call(
        functools.partial(fused_kernel, n_pos, n_obj, scale),
        out_shape=(
            jax.ShapeDtypeStruct(obj.shape, F32),
            jax.ShapeDtypeStruct(probe.shape, F32),
        ),
        in_specs=[smem, smem, smem, vmem, vmem, vmem, vmem, vmem],
        out_specs=(vmem, vmem),
        scratch_shapes=[
            pltpu.VMEM((n_pos, CAPACITY, SIZE, SIZE), BF16),
            pltpu.VMEM((n_pos, CAPACITY, SIZE, SIZE), BF16),
            pltpu.VMEM((n_pos, 8, LANES), jnp.int32),
            pltpu.VMEM((n_pos, 8, LANES), jnp.int32),
            pltpu.SMEM((n_pos, 8, LANES), jnp.int32),
            pltpu.VMEM((2, 3, 3 * SIZE, LANES), F32),
            pltpu.VMEM((2, 2, SIZE, SIZE), F32),
            pltpu.VMEM(double, BF16),
            pltpu.VMEM(double, BF16),
            pltpu.VMEM(double, F32),
            pltpu.VMEM(double, BF16),
            pltpu.VMEM(double, F32),
            pltpu.VMEM((2, 2, 3, 3 * SIZE, LANES), F32),
            pltpu.VMEM((2, 3, 2 * SIZE, LANES), F32),
            pltpu.VMEM((2, SIZE, SIZE), F32),
            pltpu.VMEM((total, 8, LANES), F32),
            pltpu.VMEM((n_obj - 1, n_pos, 8, LANES), F32),
            pltpu.VMEM((n_pos, 8, LANES), F32),
            pltpu.VMEM((n_pos - 1, 8, LANES), F32),
            pltpu.VMEM((total, 8, LANES), F32),
            dma((n_pos,)), dma((n_pos,)), dma((n_pos,)), dma((n_pos,)), dma,
            dma((count,)), dma((count,)),
        ],
        compiler_params=pltpu.CompilerParams(
            collective_id=1, has_side_effects=True, vmem_limit_bytes=56 << 20
        ),
        cost_estimate=pl.CostEstimate(
            flops=2 * n_pos * 32 * SIZE**3, bytes_accessed=16 << 20, transcendentals=0
        ),
        name="fused",
    )(owner, rows, cols, amps, obj, probe, left, right)


def exchanged(block, axis, dim):
    count = lax.axis_size(axis)
    forward = [(i, (i + 1) % count) for i in range(count)]
    backward = [(target, source) for source, target in forward]
    size = block.shape[dim]
    low = lax.ppermute(lax.slice_in_dim(block, size - 1, size, axis=dim), axis, forward)
    high = lax.ppermute(lax.slice_in_dim(block, 0, 1, axis=dim), axis, backward)
    return jnp.concatenate([low, block, high], axis=dim)


def shards(object_field, probe, amplitude, row_offset, col_offset, owner):
    n_pos = lax.axis_size("pos")
    n_obj = lax.axis_size("obj")
    pos_dev = amplitude.shape[0]
    left, right = dft_blocks()
    scale = 1.0 / math.sqrt(pos_dev * n_pos * n_obj)
    tall = exchanged(object_field, "obj", 1)
    wide = exchanged(object_field, "pos", 2)
    smooth = 4.0 * object_field - tall[:, :-2] - tall[:, 2:] - wide[:, :, :-2] - wide[:, :, 2:]
    grad, new_probe = fused(
        owner, row_offset, col_offset, amplitude, object_field, probe, left, right,
        n_pos, n_obj, scale,
    )
    return object_field - 0.25 * (grad + 0.5 * smooth), new_probe


def solution(mesh):
    placed = (
        P(None, "obj", "pos"),
        P(),
        P(("pos", "obj"), None, None),
        P(("pos", "obj")),
        P(("pos", "obj")),
        P(("pos", "obj")),
    )
    return jax.shard_map(
        shards, mesh=mesh, in_specs=placed, out_specs=(P(None, "obj", "pos"), P()), check_vma=False
    )
```

time: 180 us -> 156 us (0.87)
  Pallas kernels: 80.7 us -> 140 us
  blocking collectives: 29.8 us -> 0 us
  waiting for transfers between devices: 28.1 us -> 0.01 us
  starting transfers between devices: 22.6 us -> 8.12 us
  local copies, waits for them, and re-layouts: 15.3 us -> 2.97 us
    pallas_call x4 -> x1, Pallas kernels: 80.7 us -> 140 us  [fused(): pl.pallas_call(functools.partial(fused_kernel, n_pos, n_obj, scale), out_...]
    all_to_all x1 -> x0, blocking collectives: 29.8 us -> none  [shards(): lax.all_to_all(slots[k * n_pos:(k + 1) * n_pos], 'pos', 0, 0, tiled=True)]
    ppermute x2, waiting for transfers between devices: 23.8 us -> 0.01 us  [exchanged(): lax.ppermute(lax.slice_in_dim(block, size - 1, size, axis=dim), axis, for...]
    all_to_all x2 -> x0, starting transfers between devices: 12.5 us -> none  [the longest x1 7.58 us: shards(): lax.all_to_all(meta.reshape(CAPACITY, n_pos, 2), 'pos', 1, 1, tiled=True)]
    unnamed x13 -> x5, local copies, waits for them, and re-layouts: 7.36 us -> 0.8 us
    slice x4 -> x0, local copies, waits for them, and re-layouts: 4.2 us -> none  [the longest x1 3.94 us: shards(): slots[k * n_pos:(k + 1) * n_pos]]
    all_to_all x2 -> x0, waiting for transfers between devices: 2.51 us -> none  [the longest x1 2.51 us: shards(): lax.all_to_all(meta.reshape(CAPACITY, n_pos, 2), 'pos', 1, 1, tiled=True)]
    ppermute x2, starting transfers between devices: 6.57 us -> 4.39 us  [exchanged(): lax.ppermute(lax.slice_in_dim(block, size - 1, size, axis=dim), axis, for...]
  transfers between devices with their start and end apart: 6 -> 4, of which waited for: 3 -> 0; matrix products, arithmetic and copies ran while one was open for 5% -> 1% of each run, Pallas kernels for 13% -> 90%
where the time goes in v3:
time: 156 us
  Pallas kernels  140 us (90%)
  starting transfers between devices  8.12 us (5%)
  other arithmetic  3.64 us (2%)
  local copies, waits for them, and re-layouts  2.97 us (2%)
    pallas_call x1, Pallas kernels, fused(): pl.pallas_call(functools.partial(fused_kernel, n_pos, n_obj, scale), out_...  140 us
    ppermute x2, starting transfers between devices, exchanged(): lax.ppermute(lax.slice_in_dim(block, size - 1, size, axis=dim), axis, for...  4.39 us
    ppermute x2, starting transfers between devices, exchanged(): high = lax.ppermute(lax.slice_in_dim(block, 0, 1, axis=dim), axis, backward)  3.73 us
    sub x1, other arithmetic, shards(): return (object_field - 0.25 * (grad + 0.5 * smooth), new_probe)  3.64 us
  transfers between devices with their start and end apart: 4, of which 0 were waited for; matrix products, arithmetic and copies ran while one was open for 1% of the time, Pallas kernels for 90%

profile of v3, /device:TPU:1, one launch (start us, length us, event | category | flops | bytes accessed | tf_op | source)
XLA Modules:
  0.0 155.6 jit_solution(6368265463297765718)
XLA Ops:
  0.6 0.8 fusion.8
  1.4 3.0 %collective-permute-start = (f32[2,1,384]{2,1,0:T(1,128)S(1)}, f32[2,1,384]{2,1,0:T(1,128)S(1)}, u32[]{:S(2)}, u32[]{:S(2)}) collective-permute-start(f32[2,1,384]{2,1,0:T(1,128)S(1)} %get-tuple-element.6), channel_id=1, source_target_pairs={{0,1},{1,2},{2,3},{3,4},{4,5},{5,6},{6,7},{7,0},{8,9},{9,10},{10,1... | collective-permute-start | bytes 9224 | tf_op jit(solution)/shard_map/ppermute | solution.py:366
  4.4 0.0 collective-permute-start.1
  4.4 1.4 fusion.9
  5.8 1.4 collective-permute-start.2
  7.2 0.0 copy-start
  7.2 3.7 %collective-permute-start.3 = (f32[2,512,1]{2,1,0:T(8,128)S(1)}, f32[2,512,1]{2,1,0:T(8,128)S(1)}, u32[]{:S(2)}, u32[]{:S(2)}) collective-permute-start(f32[2,512,1]{2,1,0:T(8,128)S(1)} %get-tuple-element.9), channel_id=1, source_target_pairs={{8,0},{16,8},{24,16},{32,24},{40,32},{48,40},{56,48},{64,56},{72,6... | collective-permute-start | bytes 12296 | tf_op jit(solution)/shard_map/ppermute | solution.py:367
  10.9 140.2 %fused.1 = (f32[2,512,384]{2,1,0:T(8,128)}, f32[2,256,256]{2,1,0:T(8,128)}) custom-call(s32[16]{0:T(128)} %owner.1, s32[16]{0:T(128)} %rows.1, s32[16]{0:T(128)} %cols.1, bf16[16,256,256]{2,1,0:T(8,128)(2,1)} %amps.1, f32[2,512,384]{2,1,0:T(8,128)} %obj.1, f32[2,256,256]{2,1,0:T(8,128)} %probe.1, bf16[512,512]{1,0:T(8,128)(2,1)} %constant.21.left, ...), custom_call_target="tpu_custom_call" | custom-call | flops 17179869184 | bytes 16777216 | tf_op jit(solution)/shard_map/fused/pallas_call | solution.py:319
  151.1 0.0 collective-permute-done
  151.2 0.0 collective-permute-done.1
  151.2 0.0 collective-permute-done.2
  151.2 0.0 collective-permute-done.3
  151.2 0.0 copy-done
  151.2 0.0 copy-start.1
  151.2 3.6 %fusion.4 = f32[2,512,384]{2,1,0:T(8,128)} fusion(f32[2,512,384]{2,1,0:T(8,128)S(1)} %copy-done, f32[2,512,384]{2,1,0:T(8,128)} %get-tuple-element.4, f32[2,512,1]{2,1,0:T(8,128)S(1)} %collective-permute-done.3, f32[2,512,1]{2,1,0:T(8,128)S(1)} %collective-permute-done.2, f32[2,1,384]{2,1,0:T(1,128)S(1)} %collective-permute-done.1, ...), kind=kLoop, calls=%fused_computation.5 | loop fusion | flops 5111808 | bytes 4732928 | tf_op jit(solution)/shard_map/sub | solution.py:384
  154.8 0.0 copy-done.1
  154.8 0.8 copy.11
Async XLA Ops:
  1.4 149.8 %collective-permute-start = (f32[2,1,384]{2,1,0:T(1,128)S(1)}, f32[2,1,384]{2,1,0:T(1,128)S(1)}, u32[]{:S(2)}, u32[]{:S(2)}) collective-permute-start(f32[2,1,384]{2,1,0:T(1,128)S(1)} %get-tuple-element.6), channel_id=1, source_target_pairs={{0,1},{1,2},{2,3},{3,4},{4,5},{5,6},{6,7},{7,0},{8,9},{9,10},{10,1... | collective-permute-start | bytes 9224 | tf_op jit(solution)/shard_map/ppermute | solution.py:366
  4.4 146.7 %collective-permute-start.1 = (f32[2,1,384]{2,1,0:T(1,128)S(1)}, f32[2,1,384]{2,1,0:T(1,128)S(1)}, u32[]{:S(2)}, u32[]{:S(2)}) collective-permute-start(f32[2,1,384]{2,1,0:T(1,128)S(1)} %get-tuple-element.7), channel_id=1, source_target_pairs={{1,0},{2,1},{3,2},{4,3},{5,4},{6,5},{7,6},{0,7},{9,8},{10,9},{11,1... | collective-permute-start | bytes 9224 | tf_op jit(solution)/shard_map/ppermute | solution.py:367
  5.8 145.3 %collective-permute-start.2 = (f32[2,512,1]{2,1,0:T(8,128)S(1)}, f32[2,512,1]{2,1,0:T(8,128)S(1)}, u32[]{:S(2)}, u32[]{:S(2)}) collective-permute-start(f32[2,512,1]{2,1,0:T(8,128)S(1)} %get-tuple-element.8), channel_id=1, source_target_pairs={{0,8},{8,16},{16,24},{24,32},{32,40},{40,48},{48,56},{56,64},{64,7... | collective-permute-start | bytes 12296 | tf_op jit(solution)/shard_map/ppermute | solution.py:366
  7.2 144.0 %copy-start = (f32[2,512,384]{2,1,0:T(8,128)S(1)}, f32[2,512,384]{2,1,0:T(8,128)}, u32[]{:S(2)}) copy-start(f32[2,512,384]{2,1,0:T(8,128)} %obj.1) | copy-start | bytes 4718596
  7.2 144.0 %collective-permute-start.3 = (f32[2,512,1]{2,1,0:T(8,128)S(1)}, f32[2,512,1]{2,1,0:T(8,128)S(1)}, u32[]{:S(2)}, u32[]{:S(2)}) collective-permute-start(f32[2,512,1]{2,1,0:T(8,128)S(1)} %get-tuple-element.9), channel_id=1, source_target_pairs={{8,0},{16,8},{24,16},{32,24},{40,32},{48,40},{56,48},{64,56},{72,6... | collective-permute-start | bytes 12296 | tf_op jit(solution)/shard_map/ppermute | solution.py:367
  151.2 3.6 %copy-start.1 = (f32[2,256,256]{2,1,0:T(8,128)S(1)}, f32[2,256,256]{2,1,0:T(8,128)}, u32[]{:S(2)}) copy-start(f32[2,256,256]{2,1,0:T(8,128)} %get-tuple-element.13) | copy-start | bytes 1572868

commit v4 on v3

--- a/solution.py
+++ b/solution.py
@@ -125,22 +125,45 @@
 MESH = pl.DeviceIdType.MESH
 
 
+AHEAD = 6
+
+
+def message_order(side):
+    pending = [(x, y) for x in range(side) for y in range(side)]
+    hops = lambda d: min(d, side - d)
+
+    def rank(offset):
+        x, y = offset
+        first = min((x, y), ((side - x) % side, (side - y) % side))
+        straight = 0 if 0 in offset else 1
+        return (hops(x) + hops(y) - (hops(x) == hops(y)), straight, first)
+
+    return sorted(pending, key=rank)
+
+
 def fused_kernel(
     n_pos, n_obj, scale,
     owner, rows, cols, amps, obj, probe, left, right,
-    grad_out, probe_out,
+    object_out, probe_out,
     slots, landed, meta_out, meta_in, meta, tile, window, psi, half, wave, diff, chi, spread, acc,
-    term, tiles, got_obj, part, got_pos, done,
-    amp_send, amp_recv, meta_send, meta_recv, meta_sem, sum_send, sum_recv,
+    term, tiles, got_obj, part, got_pos, done, picked, ext, edge_out, edge_in, sides,
+    amp_send, amp_recv, meta_send, meta_recv, meta_sem, sum_send, sum_recv, halo_send, halo_recv,
 ):
     me_p = lax.axis_index("pos")
     me_o = lax.axis_index("obj")
     side = math.isqrt(n_pos)
     peer_o = [lax.rem(me_o + d, n_obj) for d in range(1, n_obj)]
 
+    order = message_order(side)
+
     def peer_at(s):
-        x = lax.rem(me_p // side + s // side, side)
-        y = lax.rem(me_p % side + s % side, side)
+        if isinstance(s, int):
+            dx, dy = order[s]
+        else:
+            dx = sum(jnp.where(s == i, d[0], 0) for i, d in enumerate(order) if d[0])
+            dy = sum(jnp.where(s == i, d[1], 0) for i, d in enumerate(order) if d[1])
+        x = lax.rem(me_p // side + dx, side)
+        y = lax.rem(me_p % side + dy, side)
         return x * side + y
 
     peer_p = [peer_at(s) for s in range(1, n_pos)]
@@ -168,7 +191,7 @@
 
     lane = lax.broadcasted_iota(jnp.int32, (8, LANES), 1)
 
-    def found(s):
+    def announce(s, corners):
         target = peer_at(s)
         first = jnp.int32(-1)
         second = jnp.int32(-1)
@@ -176,26 +199,55 @@
             hit = owner[i] == target
             second = jnp.where(hit, first, second)
             first = jnp.where(hit, i, first)
-        return first, second
-
-    def lay_out(s, out, corners):
-        picked = found(s)
         values = jnp.zeros((8, LANES), jnp.int32)
-        for k in range(CAPACITY):
-            i = jnp.maximum(picked[k], 0)
-            row = jnp.where(picked[k] < 0, 2 * SIZE, rows[i])
+        for k, found in enumerate((first, second)):
+            i = jnp.maximum(found, 0)
+            picked[s, k] = i
+            row = jnp.where(found < 0, 2 * SIZE, rows[i])
             values = jnp.where(lane == 2 * k, row, values)
             values = jnp.where(lane == 2 * k + 1, cols[i], values)
-            out[s, k] = amps[i]
         corners[s] = values
+
+    def lay_out(s, out):
+        for k in range(CAPACITY):
+            out[s, k] = amps[picked[s, k]]
 
     @pl.loop(1, n_pos)
     def _(s):
-        lay_out(s, slots, meta_out)
+        announce(s, meta_out)
         meta_copy(s).start()
+
+    @pl.loop(1, 1 + AHEAD)
+    def _(s):
+        lay_out(s, slots)
         amp_copy(s).start()
 
-    lay_out(0, landed, meta_in)
+    announce(0, meta_in)
+    lay_out(0, landed)
+
+    tall = 2 * SIZE
+    next_p, last_p = lax.rem(me_p + 1, n_pos), lax.rem(me_p + n_pos - 1, n_pos)
+    next_o, last_o = lax.rem(me_o + 1, n_obj), lax.rem(me_o + n_obj - 1, n_obj)
+
+    def halo(i, source, target, device):
+        return pltpu.make_async_remote_copy(
+            src_ref=source, dst_ref=target, send_sem=halo_send.at[i], recv_sem=halo_recv.at[i],
+            device_id=device, device_id_type=MESH,
+        )
+
+    for p in range(2):
+        edge_out[0, p] = obj[p, :, 2 * LANES : 3 * LANES].T[LANES - 8 : LANES]
+        edge_out[1, p] = obj[p, :, 0:LANES].T[0:8]
+    halos = [
+        halo(0, obj.at[:, pl.ds(tall - 8, 8), :], ext.at[:, pl.ds(0, 8), :], (me_p, next_o)),
+        halo(1, obj.at[:, pl.ds(0, 8), :], ext.at[:, pl.ds(tall + 8, 8), :], (me_p, last_o)),
+        halo(2, edge_out.at[0], edge_in.at[0], (next_p, me_o)),
+        halo(3, edge_out.at[1], edge_in.at[1], (last_p, me_o)),
+    ]
+    for c in halos:
+        c.start()
+    for p in range(2):
+        ext[p, 8 : tall + 8, :] = obj[p]
     for p in range(2):
         for k in range(3):
             block = slice(k * LANES, (k + 1) * LANES)
@@ -219,7 +271,12 @@
     def _(s):
         @pl.when(s > 0)
         def _():
-            amp_copy(s).wait()
+            amp_copy(s).wait_recv()
+
+        @pl.when(s + AHEAD + 1 < n_pos)
+        def _():
+            lay_out(s + AHEAD + 1, slots)
+            amp_copy(s + AHEAD + 1).start()
 
         row = [meta[s, 0, 2 * j] for j in range(2)]
         col = [meta[s, 0, 2 * j + 1] for j in range(2)]
@@ -236,10 +293,6 @@
             gradients(col[j], chi, probe, window, spread, term, j)
         accumulate(row, spread, acc)
 
-    for p in range(2):
-        for k in range(3):
-            grad_out[p, :, k * LANES : (k + 1) * LANES] = acc[p, k]
-
     for plane in range(2):
         for i in range(SIZE // 8):
             for k in range(2):
@@ -271,6 +324,31 @@
     copies = over_obj(0, lambda d, o: tiles.at[pl.ds(o * n_pos, n_pos)], lambda d, o: got_obj.at[d])
     for c in copies:
         c.start()
+    for c in halos:
+        c.wait()
+    middle = jnp.zeros((LANES - 16, tall), F32)
+    for p in range(2):
+        sides[p] = jnp.concatenate([edge_in[1, p], middle, edge_in[0, p]], axis=0).T
+    lanes = lax.broadcasted_iota(jnp.int32, (STRIP, LANES), 1)
+    for p in range(2):
+        for s in range(0, tall, STRIP):
+            here = [ext[p, 8 + s : 8 + s + STRIP, k * LANES : (k + 1) * LANES] for k in range(3)]
+            here.append(sides[p, s : s + STRIP, :])
+            right_of = [pltpu.roll(t, LANES - 1, 1) for t in here]
+            left_of = [pltpu.roll(t, 1, 1) for t in here]
+            for k in range(3):
+                block = slice(k * LANES, (k + 1) * LANES)
+                around = ext[p, 7 + s : 7 + s + STRIP, block] + ext[p, 9 + s : 9 + s + STRIP, block]
+                around += jnp.where(lanes == 0, left_of[k - 1], left_of[k])
+                around += jnp.where(lanes == LANES - 1, right_of[k + 1], right_of[k])
+                object_out[p, s : s + STRIP, block] = (
+                    0.5 * here[k] + 0.125 * around - 0.25 * acc[p, k, s : s + STRIP, :]
+                )
+
+    @pl.loop(1, n_pos)
+    def _(s):
+        amp_copy(s).wait_send()
+
     for c in copies:
         c.wait_recv()
     total = tiles[pl.ds(me_o * n_pos, n_pos)]
@@ -345,8 +423,13 @@
             pltpu.VMEM((n_pos, 8, LANES), F32),
             pltpu.VMEM((n_pos - 1, 8, LANES), F32),
             pltpu.VMEM((total, 8, LANES), F32),
+            pltpu.SMEM((n_pos, CAPACITY), jnp.int32),
+            pltpu.VMEM((2, 2 * SIZE + 16, 3 * LANES), F32),
+            pltpu.VMEM((2, 2, 8, 2 * SIZE), F32),
+            pltpu.VMEM((2, 2, 8, 2 * SIZE), F32),
+            pltpu.VMEM((2, 2 * SIZE, LANES), F32),
             dma((n_pos,)), dma((n_pos,)), dma((n_pos,)), dma((n_pos,)), dma,
-            dma((count,)), dma((count,)),
+            dma((count,)), dma((count,)), dma((4,)), dma((4,)),
         ],
         compiler_params=pltpu.CompilerParams(
             collective_id=1, has_side_effects=True, vmem_limit_bytes=56 << 20
@@ -358,30 +441,16 @@
     )(owner, rows, cols, amps, obj, probe, left, right)
 
 
-def exchanged(block, axis, dim):
-    count = lax.axis_size(axis)
-    forward = [(i, (i + 1) % count) for i in range(count)]
-    backward = [(target, source) for source, target in forward]
-    size = block.shape[dim]
-    low = lax.ppermute(lax.slice_in_dim(block, size - 1, size, axis=dim), axis, forward)
-    high = lax.ppermute(lax.slice_in_dim(block, 0, 1, axis=dim), axis, backward)
-    return jnp.concatenate([low, block, high], axis=dim)
-
-
 def shards(object_field, probe, amplitude, row_offset, col_offset, owner):
     n_pos = lax.axis_size("pos")
     n_obj = lax.axis_size("obj")
     pos_dev = amplitude.shape[0]
     left, right = dft_blocks()
     scale = 1.0 / math.sqrt(pos_dev * n_pos * n_obj)
-    tall = exchanged(object_field, "obj", 1)
-    wide = exchanged(object_field, "pos", 2)
-    smooth = 4.0 * object_field - tall[:, :-2] - tall[:, 2:] - wide[:, :, :-2] - wide[:, :, 2:]
-    grad, new_probe = fused(
+    return fused(
         owner, row_offset, col_offset, amplitude, object_field, probe, left, right,
         n_pos, n_obj, scale,
     )
-    return object_field - 0.25 * (grad + 0.5 * smooth), new_probe
 
 
 def solution(mesh):

time: 156 us -> 110 us (0.71)
  Pallas kernels: 140 us -> 106 us
  starting transfers between devices: 8.12 us -> 0 us
  other arithmetic: 3.64 us -> 0 us
    pallas_call x1, Pallas kernels: 140 us -> 106 us  [fused(): pl.pallas_call(functools.partial(fused_kernel, n_pos, n_obj, scale), out_...]
    ppermute x4 -> x0, starting transfers between devices: 8.12 us -> none  [the longest x2 4.39 us: exchanged(): lax.ppermute(lax.slice_in_dim(block, size - 1, size, axis=dim), axis, for...]
    sub x1 -> x0, other arithmetic: 3.64 us -> none  [shards(): return (object_field - 0.25 * (grad + 0.5 * smooth), new_probe)]
    unnamed x5 -> x4, local copies, waits for them, and re-layouts: 0.8 us -> 3.51 us
    slice x2 -> x0, local copies, waits for them, and re-layouts: 2.17 us -> none  [exchanged(): lax.slice_in_dim(block, size - 1, size, axis=dim)]
  transfers between devices with their start and end apart: 4 -> 0, of which waited for: 0 -> 0; matrix products, arithmetic and copies ran while one was open for 1% -> 0% of each run, Pallas kernels for 90% -> 0%
where the time goes in v4:
time: 110 us
  Pallas kernels  106 us (96%)
  local copies, waits for them, and re-layouts  3.51 us (3%)
    pallas_call x1, Pallas kernels, fused(): pl.pallas_call(functools.partial(fused_kernel, n_pos, n_obj, scale), out_...  106 us
    unnamed x4, local copies, waits for them, and re-layouts  3.51 us

profile of v4, /device:TPU:1, one launch (start us, length us, event | category | flops | bytes accessed | tf_op | source)
XLA Modules:
  0.0 109.9 jit_solution(3505084057206147083)
XLA Ops:
  0.6 105.7 %fused.1 = (f32[2,512,384]{2,1,0:T(8,128)}, f32[2,256,256]{2,1,0:T(8,128)}) custom-call(s32[16]{0:T(128)} %owner.1, s32[16]{0:T(128)} %rows.1, s32[16]{0:T(128)} %cols.1, bf16[16,256,256]{2,1,0:T(8,128)(2,1)} %amps.1, f32[2,512,384]{2,1,0:T(8,128)} %obj.1, f32[2,256,256]{2,1,0:T(8,128)} %probe.1, bf16[512,512]{1,0:T(8,128)(2,1)} %constant.15.left, ...), custom_call_target="tpu_custom_call" | custom-call | flops 17179869184 | bytes 16777216 | tf_op jit(solution)/shard_map/fused/pallas_call | solution.py:397
  106.4 0.0 copy-start
  106.4 2.7 %copy.12 = f32[2,512,384]{2,1,0:T(8,128)} copy(f32[2,512,384]{2,1,0:T(8,128)} %get-tuple-element.4) | data formatting | bytes 3145728
  109.1 0.0 copy-done
  109.1 0.8 copy.13
Async XLA Ops:
  106.4 2.7 %copy-start = (f32[2,256,256]{2,1,0:T(8,128)S(1)}, f32[2,256,256]{2,1,0:T(8,128)}, u32[]{:S(2)}) copy-start(f32[2,256,256]{2,1,0:T(8,128)} %get-tuple-element.5) | copy-start | bytes 1572868

commit v5 on v4

--- a/solution.py
+++ b/solution.py
@@ -125,43 +125,55 @@
 MESH = pl.DeviceIdType.MESH
 
 
-AHEAD = 6
-
-
-def message_order(side):
-    pending = [(x, y) for x in range(side) for y in range(side)]
-    hops = lambda d: min(d, side - d)
-
-    def rank(offset):
-        x, y = offset
-        first = min((x, y), ((side - x) % side, (side - y) % side))
-        straight = 0 if 0 in offset else 1
-        return (hops(x) + hops(y) - (hops(x) == hops(y)), straight, first)
-
-    return sorted(pending, key=rank)
+ORDER = (
+    (0, 0),
+    (0, 1), (0, 3), (1, 0), (3, 0),
+    (1, 2), (3, 2), (2, 0),
+    (2, 1), (2, 3), (0, 2),
+    (1, 1), (3, 3),
+    (1, 3), (3, 1),
+    (2, 2),
+)
+AT_ONCE = 4
+STARTED = (7, 7, 7, 10, 10, 12, 12, 14, 14, 15, 15, 15, 15, 15, 15, 15)
+
+
+def chosen(s, table):
+    return sum(jnp.where(s == i, v, 0) for i, v in enumerate(table) if v)
 
 
 def fused_kernel(
     n_pos, n_obj, scale,
-    owner, rows, cols, amps, obj, probe, left, right,
-    object_out, probe_out,
+    owner, rows, cols, amps_hbm, obj_hbm, probe_hbm, left_hbm, right_hbm,
+    object_hbm, probe_out,
+    amps, probe, left, right, object_out,
     slots, landed, meta_out, meta_in, meta, tile, window, psi, half, wave, diff, chi, spread, acc,
-    term, tiles, got_obj, part, got_pos, done, picked, ext, edge_out, edge_in, sides,
-    amp_send, amp_recv, meta_send, meta_recv, meta_sem, sum_send, sum_recv, halo_send, halo_recv,
+    term, exact, rounded, got_a, got_b, all_a, all_b, done, picked, ext, edge_out, edge_in, sides,
+    load_sem, amp_send, amp_recv, meta_send, meta_recv, meta_sem, sum_send, sum_recv,
+    halo_send, halo_recv, out_sem,
 ):
+    tall = 2 * SIZE
+    inner = ext.at[:, pl.ds(8, tall), :]
+    loads = [
+        pltpu.make_async_copy(source, target, load_sem.at[i])
+        for i, (source, target) in enumerate(
+            ((amps_hbm, amps), (obj_hbm, inner), (probe_hbm, probe), (left_hbm, left), (right_hbm, right))
+        )
+    ]
+    for c in loads:
+        c.start()
     me_p = lax.axis_index("pos")
     me_o = lax.axis_index("obj")
     side = math.isqrt(n_pos)
     peer_o = [lax.rem(me_o + d, n_obj) for d in range(1, n_obj)]
 
-    order = message_order(side)
 
     def peer_at(s):
         if isinstance(s, int):
-            dx, dy = order[s]
+            dx, dy = ORDER[s]
         else:
-            dx = sum(jnp.where(s == i, d[0], 0) for i, d in enumerate(order) if d[0])
-            dy = sum(jnp.where(s == i, d[1], 0) for i, d in enumerate(order) if d[1])
+            dx = chosen(s, [d[0] for d in ORDER])
+            dy = chosen(s, [d[1] for d in ORDER])
         x = lax.rem(me_p // side + dx, side)
         y = lax.rem(me_p % side + dy, side)
         return x * side + y
@@ -212,20 +224,27 @@
         for k in range(CAPACITY):
             out[s, k] = amps[picked[s, k]]
 
-    @pl.loop(1, n_pos)
+    def send(s):
+        lay_out(s, slots)
+        amp_copy(s).start()
+
+    loads[0].wait()
+
+    @pl.loop(1, 1 + AT_ONCE)
     def _(s):
         announce(s, meta_out)
         meta_copy(s).start()
-
-    @pl.loop(1, 1 + AHEAD)
+        send(s)
+
+    @pl.loop(1 + AT_ONCE, n_pos)
     def _(s):
-        lay_out(s, slots)
-        amp_copy(s).start()
+        announce(s, meta_out)
+        meta_copy(s).start()
 
     announce(0, meta_in)
     lay_out(0, landed)
-
-    tall = 2 * SIZE
+    loads[1].wait()
+
     next_p, last_p = lax.rem(me_p + 1, n_pos), lax.rem(me_p + n_pos - 1, n_pos)
     next_o, last_o = lax.rem(me_o + 1, n_obj), lax.rem(me_o + n_obj - 1, n_obj)
 
@@ -236,22 +255,20 @@
         )
 
     for p in range(2):
-        edge_out[0, p] = obj[p, :, 2 * LANES : 3 * LANES].T[LANES - 8 : LANES]
-        edge_out[1, p] = obj[p, :, 0:LANES].T[0:8]
+        edge_out[0, p] = ext[p, 8 : tall + 8, 2 * LANES : 3 * LANES].T[LANES - 8 : LANES]
+        edge_out[1, p] = ext[p, 8 : tall + 8, 0:LANES].T[0:8]
     halos = [
-        halo(0, obj.at[:, pl.ds(tall - 8, 8), :], ext.at[:, pl.ds(0, 8), :], (me_p, next_o)),
-        halo(1, obj.at[:, pl.ds(0, 8), :], ext.at[:, pl.ds(tall + 8, 8), :], (me_p, last_o)),
+        halo(0, ext.at[:, pl.ds(tall, 8), :], ext.at[:, pl.ds(0, 8), :], (me_p, next_o)),
+        halo(1, ext.at[:, pl.ds(8, 8), :], ext.at[:, pl.ds(tall + 8, 8), :], (me_p, last_o)),
         halo(2, edge_out.at[0], edge_in.at[0], (next_p, me_o)),
         halo(3, edge_out.at[1], edge_in.at[1], (last_p, me_o)),
     ]
     for c in halos:
         c.start()
     for p in range(2):
-        ext[p, 8 : tall + 8, :] = obj[p]
-    for p in range(2):
         for k in range(3):
             block = slice(k * LANES, (k + 1) * LANES)
-            tile[p, k, 0 : 2 * SIZE, :] = obj[p, :, block].astype(BF16).astype(F32)
+            tile[p, k, 0 : 2 * SIZE, :] = ext[p, 8 : tall + 8, block].astype(BF16).astype(F32)
             tile[p, k, 2 * SIZE : 3 * SIZE, :] = jnp.zeros((SIZE, LANES), F32)
             for j in range(2):
                 spread[j, p, k, 0:SIZE, :] = jnp.zeros((SIZE, LANES), F32)
@@ -266,17 +283,18 @@
     to_scalars = pltpu.make_async_copy(meta_in, meta, meta_sem)
     to_scalars.start()
     to_scalars.wait()
+    for c in loads[2:]:
+        c.wait()
 
     @pl.loop(0, n_pos)
     def _(s):
+        @pl.loop(chosen(s, (AT_ONCE,) + STARTED[:-1]) + 1, chosen(s, STARTED) + 1)
+        def _(m):
+            send(m)
+
         @pl.when(s > 0)
         def _():
             amp_copy(s).wait_recv()
-
-        @pl.when(s + AHEAD + 1 < n_pos)
-        def _():
-            lay_out(s + AHEAD + 1, slots)
-            amp_copy(s + AHEAD + 1).start()
 
         row = [meta[s, 0, 2 * j] for j in range(2)]
         col = [meta[s, 0, 2 * j + 1] for j in range(2)]
@@ -293,37 +311,43 @@
             gradients(col[j], chi, probe, window, spread, term, j)
         accumulate(row, spread, acc)
 
+    across = SIZE // LANES
     for plane in range(2):
-        for i in range(SIZE // 8):
-            for k in range(2):
-                tiles[(plane * (SIZE // 8) + i) * 2 + k] = term[
-                    plane, 8 * i : 8 * i + 8, k * LANES : (k + 1) * LANES
-                ]
-
-    def over_obj(base, source_of, target_of):
-        return [
+        for i in range(SIZE // 16):
+            for k in range(across):
+                values = term[plane, 16 * i : 16 * i + 16, k * LANES : (k + 1) * LANES]
+                exact[(plane * (SIZE // 16) + i) * across + k] = values
+                rounded[(plane * (SIZE // 16) + i) * across + k] = values.astype(BF16)
+
+    first = SIZE // 16 * across
+    a_size, b_size = first // n_obj, first // n_pos
+    of_a = lambda o: pl.ds(o * a_size, a_size)
+    of_b = lambda p: pl.ds(first + p * b_size, b_size)
+
+    def phase(base, a_of, b_of):
+        copies = []
+        for d, o in enumerate(peer_o):
+            copies.append(((me_p, o), *a_of(d, o)))
+        for d, p in enumerate(peer_p):
+            copies.append(((p, me_o), *b_of(d, p)))
+        copies = [
             pltpu.make_async_remote_copy(
-                src_ref=source_of(d, o), dst_ref=target_of(d, o),
-                send_sem=sum_send.at[base + d], recv_sem=sum_recv.at[base + d],
-                device_id=(me_p, o), device_id_type=MESH,
+                src_ref=source, dst_ref=target,
+                send_sem=sum_send.at[base + i], recv_sem=sum_recv.at[base + i],
+                device_id=device, device_id_type=MESH,
             )
-            for d, o in enumerate(peer_o)
+            for i, (device, source, target) in enumerate(copies)
         ]
-
-    def over_pos(base, source_of, target_of):
-        return [
-            pltpu.make_async_remote_copy(
-                src_ref=source_of(d, p), dst_ref=target_of(d, p),
-                send_sem=sum_send.at[base + d], recv_sem=sum_recv.at[base + d],
-                device_id=(p, me_o), device_id_type=MESH,
-            )
-            for d, p in enumerate(peer_p)
-        ]
+        for c in copies:
+            c.start()
+        return copies
 
     step = n_obj - 1 + n_pos - 1
-    copies = over_obj(0, lambda d, o: tiles.at[pl.ds(o * n_pos, n_pos)], lambda d, o: got_obj.at[d])
-    for c in copies:
-        c.start()
+    one = phase(
+        0,
+        lambda d, o: (rounded.at[of_a(o)], got_a.at[d]),
+        lambda d, p: (rounded.at[of_b(p)], got_b.at[d]),
+    )
     for c in halos:
         c.wait()
     middle = jnp.zeros((LANES - 16, tall), F32)
@@ -345,53 +369,63 @@
                     0.5 * here[k] + 0.125 * around - 0.25 * acc[p, k, s : s + STRIP, :]
                 )
 
+    pltpu.make_async_copy(object_out, object_hbm, out_sem).start()
+
     @pl.loop(1, n_pos)
     def _(s):
         amp_copy(s).wait_send()
 
-    for c in copies:
+    for c in one:
         c.wait_recv()
-    total = tiles[pl.ds(me_o * n_pos, n_pos)]
+    total = exact[of_a(me_o)]
     for d in range(n_obj - 1):
-        total += got_obj[d]
-    part[...] = total
-    second = over_pos(n_obj - 1, lambda d, p: part.at[p], lambda d, p: got_pos.at[d])
-    for c in second:
-        c.start()
-    for c in second:
+        total += got_a[d].astype(F32)
+    all_a[me_p] = total.astype(BF16)
+    total = exact[of_b(me_p)]
+    for d in range(n_pos - 1):
+        total += got_b[d].astype(F32)
+    all_b[me_o] = total.astype(BF16)
+    two = phase(
+        step,
+        lambda d, o: (all_b.at[me_o], all_b.at[me_o]),
+        lambda d, p: (all_a.at[me_p], all_a.at[me_p]),
+    )
+    for c in two:
         c.wait_recv()
-    total = part[me_p]
-    for d in range(n_pos - 1):
-        total += got_pos[d]
-    mine = me_o * n_pos + me_p
-    done[mine] = total
-    third = over_pos(step, lambda d, p: done.at[mine], lambda d, p: done.at[mine])
-    for c in third:
-        c.start()
-    for c in third:
+    total = all_a[0].astype(F32)
+    for d in range(1, n_pos):
+        total += all_a[d].astype(F32)
+    done[of_a(me_o)] = total
+    total = all_b[0].astype(F32)
+    for d in range(1, n_obj):
+        total += all_b[d].astype(F32)
+    done[of_b(me_p)] = total
+    three = phase(
+        2 * step,
+        lambda d, o: (done.at[of_a(me_o)], done.at[of_a(me_o)]),
+        lambda d, p: (done.at[of_b(me_p)], done.at[of_b(me_p)]),
+    )
+    for c in three:
         c.wait_recv()
-    block = pl.ds(me_o * n_pos, n_pos)
-    fourth = over_obj(step + n_pos - 1, lambda d, o: done.at[block], lambda d, o: done.at[block])
-    for c in fourth:
-        c.start()
-    for c in fourth:
-        c.wait_recv()
-    for c in copies + second + third + fourth:
+    for plane in range(2):
+        for i in range(SIZE // 16):
+            for k in range(across):
+                here, block = slice(16 * i, 16 * i + 16), slice(k * LANES, (k + 1) * LANES)
+                probe_out[plane, here, block] = probe[plane, here, block] - scale * done[
+                    (plane * (SIZE // 16) + i) * across + k
+                ]
+    for c in one + two + three:
         c.wait_send()
-    for plane in range(2):
-        for i in range(SIZE // 8):
-            for k in range(2):
-                here, block = slice(8 * i, 8 * i + 8), slice(k * LANES, (k + 1) * LANES)
-                probe_out[plane, here, block] = probe[plane, here, block] - scale * done[
-                    (plane * (SIZE // 8) + i) * 2 + k
-                ]
+    pltpu.make_async_copy(object_out, object_hbm, out_sem).wait()
 
 
 def fused(owner, rows, cols, amps, obj, probe, left, right, n_pos, n_obj, scale):
     smem = pl.BlockSpec(memory_space=pltpu.SMEM)
     vmem = pl.BlockSpec(memory_space=pltpu.VMEM)
-    count = 2 * (n_pos + n_obj - 2)
-    total = n_pos * n_obj
+    hbm = pl.BlockSpec(memory_space=pl.ANY)
+    count = 3 * (n_pos + n_obj - 2)
+    pieces = 2 * SIZE * SIZE // (16 * LANES)
+    a_size, b_size = pieces // 2 // n_obj, pieces // 2 // n_pos
     double = (2 * SIZE, 2 * SIZE)
     dma = pltpu.SemaphoreType.DMA
     return pl.pallas_call(
@@ -400,9 +434,14 @@
             jax.ShapeDtypeStruct(obj.shape, F32),
             jax.ShapeDtypeStruct(probe.shape, F32),
         ),
-        in_specs=[smem, smem, smem, vmem, vmem, vmem, vmem, vmem],
-        out_specs=(vmem, vmem),
+        in_specs=[smem, smem, smem, hbm, hbm, hbm, hbm, hbm],
+        out_specs=(hbm, vmem),
         scratch_shapes=[
+            pltpu.VMEM(amps.shape, BF16),
+            pltpu.VMEM(probe.shape, F32),
+            pltpu.VMEM(double, BF16),
+            pltpu.VMEM(double, BF16),
+            pltpu.VMEM(obj.shape, F32),
             pltpu.VMEM((n_pos, CAPACITY, SIZE, SIZE), BF16),
             pltpu.VMEM((n_pos, CAPACITY, SIZE, SIZE), BF16),
             pltpu.VMEM((n_pos, 8, LANES), jnp.int32),
@@ -418,18 +457,20 @@
             pltpu.VMEM((2, 2, 3, 3 * SIZE, LANES), F32),
             pltpu.VMEM((2, 3, 2 * SIZE, LANES), F32),
             pltpu.VMEM((2, SIZE, SIZE), F32),
-            pltpu.VMEM((total, 8, LANES), F32),
-            pltpu.VMEM((n_obj - 1, n_pos, 8, LANES), F32),
-            pltpu.VMEM((n_pos, 8, LANES), F32),
-            pltpu.VMEM((n_pos - 1, 8, LANES), F32),
-            pltpu.VMEM((total, 8, LANES), F32),
+            pltpu.VMEM((pieces, 16, LANES), F32),
+            pltpu.VMEM((pieces, 16, LANES), BF16),
+            pltpu.VMEM((n_obj - 1, a_size, 16, LANES), BF16),
+            pltpu.VMEM((n_pos - 1, b_size, 16, LANES), BF16),
+            pltpu.VMEM((n_pos, a_size, 16, LANES), BF16),
+            pltpu.VMEM((n_obj, b_size, 16, LANES), BF16),
+            pltpu.VMEM((pieces, 16, LANES), F32),
             pltpu.SMEM((n_pos, CAPACITY), jnp.int32),
             pltpu.VMEM((2, 2 * SIZE + 16, 3 * LANES), F32),
             pltpu.VMEM((2, 2, 8, 2 * SIZE), F32),
             pltpu.VMEM((2, 2, 8, 2 * SIZE), F32),
             pltpu.VMEM((2, 2 * SIZE, LANES), F32),
-            dma((n_pos,)), dma((n_pos,)), dma((n_pos,)), dma((n_pos,)), dma,
-            dma((count,)), dma((count,)), dma((4,)), dma((4,)),
+            dma((5,)), dma((n_pos,)), dma((n_pos,)), dma((n_pos,)), dma((n_pos,)), dma,
+            dma((count,)), dma((count,)), dma((4,)), dma((4,)), dma,
         ],
         compiler_params=pltpu.CompilerParams(
             collective_id=1, has_side_effects=True, vmem_limit_bytes=56 << 20

time: 110 us -> 98.8 us (0.90)
  Pallas kernels: 106 us -> 94.5 us
    pallas_call x1, Pallas kernels: 106 us -> 94.5 us  [fused(): pl.pallas_call(functools.partial(fused_kernel, n_pos, n_obj, scale), out_...]
where the time goes in v5:
time: 98.8 us; the launch traced here: 98.7 us
  Pallas kernels  94.5 us (96%)
  local copies, waits for them, and re-layouts  3.51 us (4%)
    pallas_call x1, Pallas kernels, fused(): pl.pallas_call(functools.partial(fused_kernel, n_pos, n_obj, scale), out_...  94.5 us
    unnamed x4, local copies, waits for them, and re-layouts  3.51 us

profile of v5, /device:TPU:1, one launch (start us, length us, event | category | flops | bytes accessed | tf_op | source)
XLA Modules:
  0.0 98.7 jit_solution(11832401909166225528)
XLA Ops:
  0.6 94.5 %fused.1 = (f32[2,512,384]{2,1,0:T(8,128)}, f32[2,256,256]{2,1,0:T(8,128)}) custom-call(s32[16]{0:T(128)} %owner.1, s32[16]{0:T(128)} %rows.1, s32[16]{0:T(128)} %cols.1, bf16[16,256,256]{2,1,0:T(8,128)(2,1)} %amps_hbm.1, f32[2,512,384]{2,1,0:T(8,128)} %obj_hbm.1, f32[2,256,256]{2,1,0:T(8,128)} %probe_hbm.1, bf16[512,512]{1,0:T(8,128)(2,1)} %constant.15.left_hbm, ...), custom_call_target="tpu_custom_call" | custom-call | flops 17179869184 | bytes 16777216 | tf_op jit(solution)/shard_map/fused/pallas_call | solution.py:431
  95.2 0.0 copy-start
  95.2 2.7 %copy.12 = f32[2,512,384]{2,1,0:T(8,128)} copy(f32[2,512,384]{2,1,0:T(8,128)} %get-tuple-element.4) | data formatting | bytes 3145728
  97.9 0.0 copy-done
  97.9 0.8 copy.13
Async XLA Ops:
  95.2 2.7 %copy-start = (f32[2,256,256]{2,1,0:T(8,128)S(1)}, f32[2,256,256]{2,1,0:T(8,128)}, u32[]{:S(2)}) copy-start(f32[2,256,256]{2,1,0:T(8,128)} %get-tuple-element.5) | copy-start | bytes 1572868

commit v6 on v5

--- a/solution.py
+++ b/solution.py
@@ -128,14 +128,13 @@
 ORDER = (
     (0, 0),
     (0, 1), (0, 3), (1, 0), (3, 0),
+    (1, 1), (3, 3), (1, 3), (3, 1),
     (1, 2), (3, 2), (2, 0),
     (2, 1), (2, 3), (0, 2),
-    (1, 1), (3, 3),
-    (1, 3), (3, 1),
     (2, 2),
 )
 AT_ONCE = 4
-STARTED = (7, 7, 7, 10, 10, 12, 12, 14, 14, 15, 15, 15, 15, 15, 15, 15)
+STARTED = (6, 6, 8, 8, 11, 11, 11, 14, 14, 14, 15, 15, 15, 15, 15, 15)
 
 
 def chosen(s, table):
@@ -145,12 +144,12 @@
 def fused_kernel(
     n_pos, n_obj, scale,
     owner, rows, cols, amps_hbm, obj_hbm, probe_hbm, left_hbm, right_hbm,
-    object_hbm, probe_out,
-    amps, probe, left, right, object_out,
+    object_out, probe_out,
+    amps, probe, left, right,
     slots, landed, meta_out, meta_in, meta, tile, window, psi, half, wave, diff, chi, spread, acc,
     term, exact, rounded, got_a, got_b, all_a, all_b, done, picked, ext, edge_out, edge_in, sides,
     load_sem, amp_send, amp_recv, meta_send, meta_recv, meta_sem, sum_send, sum_recv,
-    halo_send, halo_recv, out_sem,
+    halo_send, halo_recv,
 ):
     tall = 2 * SIZE
     inner = ext.at[:, pl.ds(8, tall), :]
@@ -369,7 +368,6 @@
                     0.5 * here[k] + 0.125 * around - 0.25 * acc[p, k, s : s + STRIP, :]
                 )
 
-    pltpu.make_async_copy(object_out, object_hbm, out_sem).start()
 
     @pl.loop(1, n_pos)
     def _(s):
@@ -416,7 +414,6 @@
                 ]
     for c in one + two + three:
         c.wait_send()
-    pltpu.make_async_copy(object_out, object_hbm, out_sem).wait()
 
 
 def fused(owner, rows, cols, amps, obj, probe, left, right, n_pos, n_obj, scale):
@@ -431,17 +428,16 @@
     return pl.pallas_call(
         functools.partial(fused_kernel, n_pos, n_obj, scale),
         out_shape=(
-            jax.ShapeDtypeStruct(obj.shape, F32),
-            jax.ShapeDtypeStruct(probe.shape, F32),
+            pltpu.VMEM(obj.shape, F32),
+            pltpu.VMEM(probe.shape, F32),
         ),
         in_specs=[smem, smem, smem, hbm, hbm, hbm, hbm, hbm],
-        out_specs=(hbm, vmem),
+        out_specs=(vmem, vmem),
         scratch_shapes=[
             pltpu.VMEM(amps.shape, BF16),
             pltpu.VMEM(probe.shape, F32),
             pltpu.VMEM(double, BF16),
             pltpu.VMEM(double, BF16),
-            pltpu.VMEM(obj.shape, F32),
             pltpu.VMEM((n_pos, CAPACITY, SIZE, SIZE), BF16),
             pltpu.VMEM((n_pos, CAPACITY, SIZE, SIZE), BF16),
             pltpu.VMEM((n_pos, 8, LANES), jnp.int32),
@@ -470,10 +466,10 @@
             pltpu.VMEM((2, 2, 8, 2 * SIZE), F32),
             pltpu.VMEM((2, 2 * SIZE, LANES), F32),
             dma((5,)), dma((n_pos,)), dma((n_pos,)), dma((n_pos,)), dma((n_pos,)), dma,
-            dma((count,)), dma((count,)), dma((4,)), dma((4,)), dma,
+            dma((count,)), dma((count,)), dma((4,)), dma((4,)),
         ],
         compiler_params=pltpu.CompilerParams(
-            collective_id=1, has_side_effects=True, vmem_limit_bytes=56 << 20
+            collective_id=1, has_side_effects=True, vmem_limit_bytes=52 << 20
         ),
         cost_estimate=pl.CostEstimate(
             flops=2 * n_pos * 32 * SIZE**3, bytes_accessed=16 << 20, transcendentals=0

time: 98.8 us -> 92.8 us (0.939)
  Pallas kernels: 94.5 us -> 90 us
  local copies, waits for them, and re-layouts: 3.51 us -> 1.94 us
    pallas_call x1, Pallas kernels: 94.5 us -> 90 us  [fused(): pl.pallas_call(functools.partial(fused_kernel, n_pos, n_obj, scale), out_...]
    unnamed x4 -> x2, local copies, waits for them, and re-layouts: 3.51 us -> 1.94 us
where the time goes in v6:
time: 92.8 us; the launch traced here: 92.5 us
  Pallas kernels  90 us (97%)
  local copies, waits for them, and re-layouts  1.94 us (2%)
    pallas_call x1, Pallas kernels, fused(): pl.pallas_call(functools.partial(fused_kernel, n_pos, n_obj, scale), out_...  90 us
    unnamed x2, local copies, waits for them, and re-layouts  1.94 us

profile of v6, /device:TPU:1, one launch (start us, length us, event | category | flops | bytes accessed | tf_op | source)
XLA Modules:
  0.0 92.5 jit_solution(7732335500256670773)
XLA Ops:
  0.6 90.0 %fused.1 = (f32[2,512,384]{2,1,0:T(8,128)S(1)}, f32[2,256,256]{2,1,0:T(8,128)S(1)}) custom-call(s32[16]{0:T(128)} %owner.1, s32[16]{0:T(128)} %rows.1, s32[16]{0:T(128)} %cols.1, bf16[16,256,256]{2,1,0:T(8,128)(2,1)} %amps_hbm.1, f32[2,512,384]{2,1,0:T(8,128)} %obj_hbm.1, f32[2,256,256]{2,1,0:T(8,128)} %probe_hbm.1, bf16[512,512]{1,0:T(8,128)(2,1)} %constant.15.left_hbm, ...), custom_call_target="tpu_custom_call" | custom-call | flops 17179869184 | bytes 16777216 | tf_op jit(solution)/shard_map/fused/pallas_call | solution.py:428
  90.6 1.1 %copy.12 = f32[2,512,384]{2,1,0:T(8,128)} copy(f32[2,512,384]{2,1,0:T(8,128)S(1)} %get-tuple-element.2) | data formatting | bytes 3145728
  91.7 0.8 copy.13

commit v7 on v6

--- a/solution.py
+++ b/solution.py
@@ -134,7 +134,7 @@
     (2, 2),
 )
 AT_ONCE = 4
-STARTED = (6, 6, 8, 8, 11, 11, 11, 14, 14, 14, 15, 15, 15, 15, 15, 15)
+STARTED = (6, 6, 8, 8, 11, 11, 11, 14, 15, 15, 15, 15, 15, 15, 15, 15)
 
 
 def chosen(s, table):
@@ -293,6 +293,7 @@
 
         @pl.when(s > 0)
         def _():
+            accumulate([meta[s - 1, 0, 2 * j] for j in range(2)], spread, acc)
             amp_copy(s).wait_recv()
 
         row = [meta[s, 0, 2 * j] for j in range(2)]
@@ -308,7 +309,6 @@
         chi[...] = jnp.dot(half[...], left[...], preferred_element_type=F32)
         for j in range(2):
             gradients(col[j], chi, probe, window, spread, term, j)
-        accumulate(row, spread, acc)
 
     across = SIZE // LANES
     for plane in range(2):
@@ -325,10 +325,10 @@
 
     def phase(base, a_of, b_of):
         copies = []
-        for d, o in enumerate(peer_o):
+        for d, p in reversed(list(enumerate(peer_p))) if b_of else ():
+            copies.append(((p, me_o), *b_of(d, p)))
+        for d, o in enumerate(peer_o) if a_of else ():
             copies.append(((me_p, o), *a_of(d, o)))
-        for d, p in enumerate(peer_p):
-            copies.append(((p, me_o), *b_of(d, p)))
         copies = [
             pltpu.make_async_remote_copy(
                 src_ref=source, dst_ref=target,
@@ -347,6 +347,7 @@
         lambda d, o: (rounded.at[of_a(o)], got_a.at[d]),
         lambda d, p: (rounded.at[of_b(p)], got_b.at[d]),
     )
+    accumulate([meta[n_pos - 1, 0, 2 * j] for j in range(2)], spread, acc)
     for c in halos:
         c.wait()
     middle = jnp.zeros((LANES - 16, tall), F32)
@@ -373,37 +374,37 @@
     def _(s):
         amp_copy(s).wait_send()
 
-    for c in one:
+    for c in one[n_pos - 1 :]:
         c.wait_recv()
     total = exact[of_a(me_o)]
     for d in range(n_obj - 1):
         total += got_a[d].astype(F32)
     all_a[me_p] = total.astype(BF16)
+    two = phase(step, None, lambda d, p: (all_a.at[me_p], all_a.at[me_p]))
+    for c in one[: n_pos - 1]:
+        c.wait_recv()
     total = exact[of_b(me_p)]
     for d in range(n_pos - 1):
         total += got_b[d].astype(F32)
     all_b[me_o] = total.astype(BF16)
-    two = phase(
-        step,
-        lambda d, o: (all_b.at[me_o], all_b.at[me_o]),
-        lambda d, p: (all_a.at[me_p], all_a.at[me_p]),
-    )
+    more = phase(step + n_pos - 1, lambda d, o: (all_b.at[me_o], all_b.at[me_o]), None)
+    for c in more:
+        c.wait_recv()
+    total = all_b[0].astype(F32)
+    for d in range(1, n_obj):
+        total += all_b[d].astype(F32)
+    done[of_b(me_p)] = total
+    three = phase(2 * step, None, lambda d, p: (done.at[of_b(me_p)], done.at[of_b(me_p)]))
     for c in two:
         c.wait_recv()
     total = all_a[0].astype(F32)
     for d in range(1, n_pos):
         total += all_a[d].astype(F32)
     done[of_a(me_o)] = total
-    total = all_b[0].astype(F32)
-    for d in range(1, n_obj):
-        total += all_b[d].astype(F32)
-    done[of_b(me_p)] = total
-    three = phase(
-        2 * step,
-        lambda d, o: (done.at[of_a(me_o)], done.at[of_a(me_o)]),
-        lambda d, p: (done.at[of_b(me_p)], done.at[of_b(me_p)]),
+    last = phase(
+        2 * step + n_pos - 1, lambda d, o: (done.at[of_a(me_o)], done.at[of_a(me_o)]), None
     )
-    for c in three:
+    for c in three + last:
         c.wait_recv()
     for plane in range(2):
         for i in range(SIZE // 16):
@@ -412,7 +413,7 @@
                 probe_out[plane, here, block] = probe[plane, here, block] - scale * done[
                     (plane * (SIZE // 16) + i) * across + k
                 ]
-    for c in one + two + three:
+    for c in one + two + more + three + last:
         c.wait_send()
 
 

time: 92.8 us -> 91 us (0.981)
  Pallas kernels: 90 us -> 88.3 us
    pallas_call x1, Pallas kernels: 90 us -> 88.3 us  [fused(): pl.pallas_call(functools.partial(fused_kernel, n_pos, n_obj, scale), out_...]
where the time goes in v7:
time: 91 us; the launch traced here: 90.9 us
  Pallas kernels  88.3 us (97%)
  local copies, waits for them, and re-layouts  1.94 us (2%)
    pallas_call x1, Pallas kernels, fused(): pl.pallas_call(functools.partial(fused_kernel, n_pos, n_obj, scale), out_...  88.3 us
    unnamed x2, local copies, waits for them, and re-layouts  1.94 us

profile of v7, /device:TPU:1, one launch (start us, length us, event | category | flops | bytes accessed | tf_op | source)
XLA Modules:
  0.0 90.9 jit_solution(4090962016036643103)
XLA Ops:
  0.6 88.3 %fused.1 = (f32[2,512,384]{2,1,0:T(8,128)S(1)}, f32[2,256,256]{2,1,0:T(8,128)S(1)}) custom-call(s32[16]{0:T(128)} %owner.1, s32[16]{0:T(128)} %rows.1, s32[16]{0:T(128)} %cols.1, bf16[16,256,256]{2,1,0:T(8,128)(2,1)} %amps_hbm.1, f32[2,512,384]{2,1,0:T(8,128)} %obj_hbm.1, f32[2,256,256]{2,1,0:T(8,128)} %probe_hbm.1, bf16[512,512]{1,0:T(8,128)(2,1)} %constant.15.left_hbm, ...), custom_call_target="tpu_custom_call" | custom-call | flops 17179869184 | bytes 16777216 | tf_op jit(solution)/shard_map/fused/pallas_call | solution.py:429
  89.0 1.1 %copy.12 = f32[2,512,384]{2,1,0:T(8,128)} copy(f32[2,512,384]{2,1,0:T(8,128)S(1)} %get-tuple-element.2) | data formatting | bytes 3145728
  90.1 0.8 copy.13
